TPU v7x, 32 devices: a whole 2x2x4 slice. The times are simulated.
32 devices in a mesh: gx: 32 (over z, y, x, core).
Axes of the slice: x: 2, y: 2, z: 4, core: 2. Of those that a mesh axis runs over, the one named last changes fastest.
Arguments:
- hot_cache: bfloat16 [16384, 128], P('gx'), may hold values from -6 to 6
- cold_table: bfloat16 [262144, 128], P('gx'), may hold values from -6 to 6
- serve_index: int32 [32, 32, 32], P('gx'), may hold values from 0 to 8191
- serve_count: int32 [32, 32], P('gx'), may hold values from 1 to 32, as said below
- target_slot: int32 [4096, 11], P('gx'), may hold values from 0 to 17407, as said below
- hop2_slot: int32 [4096, 11, 15], P('gx'), may hold values from 0 to 17407, as said below
- hop1_count: int32 [4096], P('gx'), may hold values from 1 to 10
- hop2_count: int32 [4096, 11], P('gx'), may hold values from 1 to 15
- w_first: bfloat16 [256, 256], replicated, may hold values from -0.375 to 0.375
- b_first: float32 [256], replicated, may hold values from -3 to 3
- w_second: bfloat16 [512, 256], replicated, may hold values from -0.25 to 0.25
- b_second: float32 [256], replicated, may hold values from -3 to 3
Outputs:
- embedding: float32 [4096, 256], P('gx')
Inputs may be any that keep to these rules, and one draw needn't show every extreme that they name: `serve_count`: live cold slots from owner o to device d; for every draw some owner sends 32 live rows to every device. A slot below 16384 is a hot-cache row, owned by device slot // 512; otherwise it is 16384 + o * 32 + j with j < serve_count[o, d], d the seed's device. Over all entries of target_slot and hop2_slot of one device's seeds, at most 64 distinct hot rows of any one owner appear, and some owner has exactly 64 for every device. `hop2_slot`: as target_slot.
All inputs are finite; a program needn't handle non-finite values.
Results may differ from a plain program's by a relative error of at most 0.0024.
Values may be sent and summed in bfloat16 or wider, within the bound.
No kernel may reach another device: no remote copies, remote signals or barrier semaphores. Data moves between devices by JAX's collectives and lax.ppermute only.
A program may use at most 128 MiB of HBM per device.

v0:
```python
import jax
import jax.numpy as jnp
from jax import lax
from jax.sharding import PartitionSpec as P


def pick_rows(table, offset, own_slot, near_slot, live):
    size = table.shape[0]
    empty = jnp.zeros((), table.dtype)
    own_local = own_slot - offset
    own_inside = (own_local >= 0) & (own_local < size)
    own_picked = table[jnp.clip(own_local, 0, size - 1)]
    own_rows = jnp.where(own_inside[..., None], own_picked, empty).astype(jnp.float32)
    near_local = near_slot - offset
    near_inside = (near_local >= 0) & (near_local < size) & live
    near_picked = table[jnp.clip(near_local, 0, size - 1)]
    near_rows = jnp.where(near_inside[..., None], near_picked, empty)
    neighbour_sum = jnp.sum(near_rows.astype(jnp.float32), axis=2)
    return (own_rows, neighbour_sum)


def layers(own_rows, neighbour_sum, hop1_count, hop2_count, w_first, b_first, w_second, b_second):
    aggregate = (neighbour_sum / hop2_count[..., None].astype(jnp.float32)).astype(jnp.bfloat16)
    stacked = jnp.concatenate([own_rows.astype(jnp.bfloat16), aggregate], -1)
    seed_rows, targets_here = (stacked.shape[0], stacked.shape[1])
    hidden = (
        jnp.dot(
            stacked.reshape(seed_rows * targets_here, -1),
            w_first,
            preferred_element_type=jnp.float32,
        )
        + b_first
    )
    hidden = jax.nn.relu(hidden).astype(jnp.bfloat16).reshape(seed_rows, targets_here, -1)
    first_mask = (
        lax.broadcasted_iota(jnp.int32, (seed_rows, targets_here - 1), 1) < hop1_count[:, None]
    ).astype(jnp.bfloat16)
    pooled = jnp.einsum(
        "bjh,bj->bh", hidden[:, 1:], first_mask, preferred_element_type=jnp.float32
    ) / hop1_count[:, None].astype(jnp.float32)
    joined = jnp.concatenate([hidden[:, 0], pooled.astype(jnp.bfloat16)], -1)
    return jnp.dot(joined, w_second, preferred_element_type=jnp.float32) + b_second


def on_device(
    hot_cache,
    cold_table,
    serve_index,
    serve_count,
    target_slot,
    hop2_slot,
    hop1_count,
    hop2_count,
    w_first,
    b_first,
    w_second,
    b_second,
):
    served_index = serve_index[0]
    live_counts = serve_count[0]
    slot_iota = lax.broadcasted_iota(jnp.int32, served_index.shape, 1)
    served = cold_table[served_index]
    served = jnp.where(
        (slot_iota < live_counts[:, None])[..., None], served, jnp.zeros((), cold_table.dtype)
    )
    received = lax.all_to_all(served, "gx", split_axis=0, concat_axis=0, tiled=True)
    cold_block = received.reshape(-1, received.shape[2])
    live = lax.broadcasted_iota(jnp.int32, hop2_slot.shape, 2) < hop2_count[..., None]
    hot_all = lax.all_gather(hot_cache, "gx", axis=0, tiled=True)
    table = jnp.concatenate([hot_all, cold_block], 0)
    own_rows, neighbour_sum = pick_rows(table, 0, target_slot, hop2_slot, live)
    return layers(
        own_rows, neighbour_sum, hop1_count, hop2_count, w_first, b_first, w_second, b_second
    )


def solution(mesh):
    return jax.shard_map(
        on_device,
        mesh=mesh,
        in_specs=(
            P("gx", None),
            P("gx", None),
            P("gx", None, None),
            P("gx", None),
            P("gx", None),
            P("gx", None, None),
            P("gx"),
            P("gx", None),
            P(),
            P(),
            P(),
            P(),
        ),
        out_specs=P("gx", None),
        check_vma=False,
    )
```

profile of v0, /device:TPU:0, one launch (start us, length us, event | category | flops | bytes accessed | tf_op | source)
XLA Modules:
  0.0 165.7 jit_solution(1542679311721152245)
XLA Ops:
  6.5 0.0 copy-start
  6.5 0.0 copy-start.4
  6.5 0.0 copy-start.1
  6.5 0.0 all-gather.2.cloned.1.call-start
  6.5 0.7 all-gather.2.cloned.1.call-update
  7.3 0.7 compare_select_fusion.1
  8.0 0.1 reshape.79
  8.1 0.1 copy-done
  8.2 3.2 %gather_fusion = bf16[1024,128]{1,0:T(8,128)(2,1)S(1)} fusion(bf16[8192,128]{1,0:T(8,128)(2,1)S(1)} %copy-done, s32[1024]{0:T(1024)S(1)} %broadcast_clamp_fusion), kind=kCustom, calls=%fused_computation | custom fusion | bytes 528384 | tf_op jit(solution)/shard_map/gather | solution.py:62
  11.4 0.7 iota_compare_fusion.2
  12.1 0.9 broadcast_select_fusion.1
  13.0 7.3 %all-to-all-start = ((bf16[32,32,128]{2,1,0:T(8,128)(2,1)}), bf16[32,32,128]{2,1,0:T(8,128)(2,1)S(1)}, u32[]{:S(2)}, u32[]{:S(2)}) async-start(bf16[32,32,128]{2,1,0:T(8,128)(2,1)} %broadcast_select_fusion.1), calls=%async_computation | async-start | bytes 524288 | tf_op jit(solution)/shard_map/all_to_all | solution.py:66
  20.4 0.7 convert_element_type.28
  21.0 0.7 convert_element_type.25
  21.7 0.7 compare_and_fusion
  22.4 0.1 copy.14
  22.6 0.2 broadcast_in_dim.54
  22.8 0.1 copy.18
  22.9 0.2 div.19
  23.1 0.7 compare_select_fusion.2
  23.8 0.1 copy.15
  23.9 0.2 reshape.87
  24.1 0.9 fusion.12
  25.0 1.2 copy.16
  26.2 0.0 copy-done.1
  26.3 0.5 copy.17
  26.8 0.4 reshape.95
  27.2 0.0 copy-done.4
  27.2 0.1 fusion.13
  27.3 5.8 %all-to-all-done = bf16[32,32,128]{2,1,0:T(8,128)(2,1)S(1)} async-done(((bf16[32,32,128]{2,1,0:T(8,128)(2,1)}), bf16[32,32,128]{2,1,0:T(8,128)(2,1)S(1)}, u32[]{:S(2)}, u32[]{:S(2)}) %all-to-all-start) | async-done | bytes 262176 | tf_op jit(solution)/shard_map/all_to_all | solution.py:66
  33.1 42.6 %all-gather.2.cloned.1.call-done = bf16[16384,128]{1,0:T(8,128)(2,1)} async-done(((bf16[512,128]{1,0:T(8,128)(2,1)}), bf16[16384,128]{1,0:T(8,128)(2,1)}) %all-gather.2.cloned.1.call-update) | async-done | bytes 4194320 | tf_op jit(solution)/shard_map/all_gather | solution.py:69
  75.7 11.8 %pad_maximum_fusion = bf16[17408,128]{1,0:T(8,128)(2,1)} fusion(bf16[1024,128]{1,0:T(8,128)(2,1)S(1)} %bitcast.18, bf16[16384,128]{1,0:T(8,128)(2,1)} %all-gather.2.cloned.1.call-done), kind=kLoop, calls=%fused_computation.4 | loop fusion | flops 8912896 | bytes 8912896 | tf_op jit(solution)/shard_map/concatenate | solution.py:70
  87.5 5.6 %gather_fusion.1 = bf16[1408,128]{1,0:T(8,128)(2,1)S(1)} fusion(bf16[17408,128]{1,0:T(8,128)(2,1)} %pad_maximum_fusion, s32[2048]{0:T(1024)S(1)} %pad_clamp_fusion.1), kind=kCustom, calls=%fused_computation.1 | custom fusion | bytes 726528 | tf_op jit(solution)/shard_map/gather | solution.py:12
  93.1 42.6 %gather_fusion.2 = bf16[21120,128]{1,0:T(8,128)(2,1)} fusion(bf16[17408,128]{1,0:T(8,128)(2,1)} %pad_maximum_fusion, s32[21504]{0:T(1024)S(1)} %pad_clamp_fusion), kind=kCustom, calls=%fused_computation.2 | custom fusion | bytes 10897920 | tf_op jit(solution)/shard_map/gather | solution.py:16
  135.7 9.2 %reshape.94 = bf16[128,11,15,128]{3,2,1,0:T(8,128)(2,1)} reshape(bf16[21120,128]{1,0:T(8,128)(2,1)} %gather_fusion.2) | data formatting | bytes 10813440 | tf_op jit(solution)/shard_map/gather | solution.py:16
  144.9 0.0 copy-start.5
  144.9 6.3 %convert_reduce_fusion = f32[128,11,128]{2,1,0:T(8,128)S(1)} fusion(bf16[128,11,15,128]{3,2,1,0:T(8,128)(2,1)} %reshape.94, pred[128,11,15]{2,1,0:T(8,128)(4,1)} %copy.16), kind=kLoop, calls=%fused_computation.3 | loop fusion | flops 7929856 | bytes 6148736 | tf_op jit(solution)/shard_map/reduce_sum | solution.py:18
  151.2 0.9 reduce_sum.12
  152.2 0.0 copy-start.3
  152.2 0.3 broadcast_select_fusion
  152.4 0.0 copy-start.2
  152.5 1.4 divide_convert_fusion
  153.9 0.0 copy-done.5
  153.9 2.1 %fusion.1 = bf16[1408,256]{1,0:T(8,128)(2,1)} fusion(bf16[256,256]{1,0:T(8,128)(2,1)} %param.20, bf16[1408,128]{1,0:T(8,128)(2,1)S(1)} %divide_convert_fusion, bf16[1408,128]{1,0:T(8,128)(2,1)S(1)} %broadcast_select_fusion, f32[256]{0:T(256)S(1)} %copy-done.5), kind=kOutput, calls=%fused_computation.7 | convolution fusion | flops 187072512 | bytes 1573888 | tf_op jit(solution)/shard_map/dot_general | solution.py:27
  156.0 1.3 reshape.76
  157.3 0.1 slice.14
  157.4 0.4 fusion.2
  157.9 0.1 fusion.11
  158.0 0.0 copy-done.3
  158.0 0.0 copy-done.2
  158.0 0.8 convolution_add_fusion.1
  (5 shorter events, 0.1 us)
Async XLA Ops:
  6.5 1.6 copy-start
  6.5 20.6 %copy-start.4 = (s32[128]{0:T(128)S(1)}, s32[128]{0:T(128)}, u32[]{:S(2)}) copy-start(s32[128]{0:T(128)} %param.18) | copy-start | bytes 1540
  6.5 19.7 %copy-start.1 = (s32[128,11,15]{0,2,1:T(8,128)S(1)}, s32[128,11,15]{0,2,1:T(8,128)}, u32[]{:S(2)}) copy-start(s32[128,11,15]{0,2,1:T(8,128)} %param.17) | copy-start | bytes 253444
  6.5 69.1 %all-gather.2.cloned.1.call-start = ((), (), s32[]{:S(2)}) async-start(), calls=%async_computation.1 | async-start | bytes 4325376 | tf_op jit(solution)/shard_map/all_gather | solution.py:69
  13.0 20.0 %all-to-all-start = ((bf16[32,32,128]{2,1,0:T(8,128)(2,1)}), bf16[32,32,128]{2,1,0:T(8,128)(2,1)S(1)}, u32[]{:S(2)}, u32[]{:S(2)}) async-start(bf16[32,32,128]{2,1,0:T(8,128)(2,1)} %broadcast_select_fusion.1), calls=%async_computation | async-start | bytes 524288 | tf_op jit(solution)/shard_map/all_to_all | solution.py:66
  144.9 9.0 %copy-start.5 = (f32[256]{0:T(256)S(1)}, f32[256]{0:T(256)}, u32[]{:S(2)}) copy-start(f32[256]{0:T(256)} %param.21) | copy-start | bytes 3076
  152.2 5.8 %copy-start.3 = (f32[256]{0:T(256)S(1)}, f32[256]{0:T(256)}, u32[]{:S(2)}) copy-start(f32[256]{0:T(256)} %param.23) | copy-start | bytes 3076
  152.4 5.5 %copy-start.2 = (bf16[512,256]{1,0:T(8,128)(2,1)S(1)}, bf16[512,256]{1,0:T(8,128)(2,1)}, u32[]{:S(2)}) copy-start(bf16[512,256]{1,0:T(8,128)(2,1)} %param.22) | copy-start | bytes 786436
Sparse Core Ops, SparseCore 0:
  10.2 65.4 all-gather.1
where the time goes:
time: 166 us
  local copies, waits for them, and re-layouts  66.2 us (40%)
  waiting for transfers between devices  49.1 us (30%)
  other arithmetic  26.1 us (16%)
  between operations  13.6 us (8%)
  starting transfers between devices  7.33 us (4%)
  matrix products  3.41 us (2%)
    gather x2, local copies, waits for them, and re-layouts, pick_rows(): near_picked = table[jnp.clip(near_local, 0, size - 1)]  51.8 us
    all_gather x1, waiting for transfers between devices, on_device(): hot_all = lax.all_gather(hot_cache, 'gx', axis=0, tiled=True)  42.6 us
    concatenate x1, other arithmetic, on_device(): table = jnp.concatenate([hot_all, cold_block], 0)  11.8 us
    all_to_all x1, starting transfers between devices, on_device(): lax.all_to_all(served, 'gx', split_axis=0, concat_axis=0, tiled=True)  7.33 us
    reduce_sum x1, other arithmetic, pick_rows(): neighbour_sum = jnp.sum(near_rows.astype(jnp.float32), axis=2)  6.33 us
    all_to_all x1, waiting for transfers between devices, on_device(): lax.all_to_all(served, 'gx', split_axis=0, concat_axis=0, tiled=True)  5.77 us
    gather x1, local copies, waits for them, and re-layouts, pick_rows(): own_picked = table[jnp.clip(own_local, 0, size - 1)]  5.62 us
  transfers between devices with their start and end apart: 2, of which 2 were waited for; matrix products, arithmetic and copies ran while one was open for 8% of the time, Pallas kernels for 0%

commit v1 on v0

v1 whole, which is shorter than its diff:
```python
import functools

import jax
import jax.numpy as jnp
from jax import lax
from jax.experimental import pallas as pl
from jax.experimental.pallas import tpu as pltpu
from jax.sharding import PartitionSpec as P


def finish_kernel(
    slots, hop1, hot, cold, count_two, count_one, w_first, b_first, w_second, b_second,
    out, table, own, total, stage, sems,
):
    n_hot, n_cold = hot.shape[0], cold.shape[0]
    seeds, width = own.shape[1:]
    targets = count_two.shape[1]
    group = 2
    per = slots.shape[0] // (own.shape[0] * seeds)
    block = stage.shape[1]
    pieces = [(hot, i) for i in range(0, n_hot, block)]
    pieces += [(cold, i) for i in range(0, n_cold, block)]

    def fetch(p):
        ref, start = pieces[p]
        return pltpu.make_async_copy(
            ref.at[pl.ds(start, block)], stage.at[p % 2], sems.at[p % 2]
        )

    fetch(0).start()
    table[pl.ds(n_hot + n_cold, 8), :] = jnp.zeros((8, width), jnp.float32)
    for p in range(len(pieces)):
        if p + 1 < len(pieces):
            fetch(p + 1).start()
        fetch(p).wait()
        table[pl.ds(p * block, block), :] = stage[p % 2].astype(jnp.float32)

    def tree(rows):
        while len(rows) > 1:
            rows = [a + b for a, b in zip(rows[::2], rows[1::2])] + (
                [rows[-1]] if len(rows) % 2 else []
            )
        return rows[0]

    def one_seed(s, carry):
        def some_targets(i, inner):
            first = i * group
            base = first * (per * seeds) + s
            for g in range(group):
                near = [
                    table[pl.ds(slots[base + ((g * per + k) * seeds)], 1), :] for k in range(per)
                ]
                own[first + g, pl.ds(s, 1), :] = near[0]
                total[first + g, pl.ds(s, 1), :] = tree(near[1:])
            return inner

        return lax.fori_loop(0, (hop1[s] + group) // group, some_targets, carry)

    lax.fori_loop(0, seeds, one_seed, 0)

    pooled = jnp.zeros((seeds, w_first.shape[1]), jnp.float32)
    near = count_one[...]
    for t in range(targets):
        aggregate = (total[t] / count_two[:, t : t + 1].astype(jnp.float32)).astype(jnp.bfloat16)
        stacked = jnp.concatenate([own[t].astype(jnp.bfloat16), aggregate], -1)
        hidden = jnp.dot(stacked, w_first[...], preferred_element_type=jnp.float32) + b_first[...]
        hidden = jnp.maximum(hidden, 0.0).astype(jnp.bfloat16)
        if t == 0:
            seed_hidden = hidden
        else:
            pooled += jnp.where(near > t - 1, hidden.astype(jnp.float32), 0.0)
    pooled = (pooled / near.astype(jnp.float32)).astype(jnp.bfloat16)
    joined = jnp.concatenate([seed_hidden, pooled], -1)
    out[...] = jnp.dot(joined, w_second[...], preferred_element_type=jnp.float32) + b_second[...]


def finish(hot, cold, slots, hop1, hop2, w_first, b_first, w_second, b_second):
    seeds, targets = hop2.shape
    width = hot.shape[1]
    rows = hot.shape[0] + cold.shape[0]
    block = cold.shape[0]
    vmem = pl.BlockSpec(memory_space=pltpu.VMEM)
    smem = pl.BlockSpec(memory_space=pltpu.SMEM)
    anyspace = pl.BlockSpec(memory_space=pl.ANY)
    return pl.pallas_call(
        finish_kernel,
        out_shape=jax.ShapeDtypeStruct((seeds, w_second.shape[1]), jnp.float32),
        in_specs=[smem, smem, anyspace, anyspace] + [vmem] * 6,
        out_specs=vmem,
        scratch_shapes=[
            pltpu.VMEM((rows + 8, width), jnp.float32),
            pltpu.VMEM((targets + targets % 2, seeds, width), jnp.float32),
            pltpu.VMEM((targets + targets % 2, seeds, width), jnp.float32),
            pltpu.VMEM((2, block, width), hot.dtype),
            pltpu.SemaphoreType.DMA((2,)),
        ],
        name="finish",
    )(
        slots, hop1, hot, cold, hop2, hop1[:, None],
        w_first, b_first[None], w_second, b_second[None],
    )


def on_device(
    hot_cache, cold_table, serve_index, serve_count, target_slot, hop2_slot,
    hop1_count, hop2_count, w_first, b_first, w_second, b_second,
):
    served_index = serve_index[0]
    live_counts = serve_count[0]
    slot_iota = lax.broadcasted_iota(jnp.int32, served_index.shape, 1)
    served = cold_table[served_index]
    served = jnp.where(
        (slot_iota < live_counts[:, None])[..., None], served, jnp.zeros((), cold_table.dtype)
    )
    received = lax.all_to_all(served, "gx", split_axis=0, concat_axis=0, tiled=True)
    cold_block = received.reshape(-1, received.shape[2])
    hot_all = lax.all_gather(hot_cache, "gx", axis=0, tiled=True)
    empty_row = hot_all.shape[0] + cold_block.shape[0]
    near = jnp.transpose(hop2_slot, (1, 2, 0))
    live = lax.broadcasted_iota(jnp.int32, near.shape, 1) < hop2_count.T[:, None, :]
    slots = jnp.concatenate([target_slot.T[:, None, :], jnp.where(live, near, empty_row)], 1)
    slots = jnp.pad(slots, ((0, slots.shape[0] % 2), (0, 0), (0, 0))).reshape(-1)
    return finish(
        hot_all, cold_block, slots, hop1_count, hop2_count, w_first, b_first, w_second, b_second
    )


def solution(mesh):
    return jax.shard_map(
        on_device,
        mesh=mesh,
        in_specs=(
            P("gx", None), P("gx", None), P("gx", None, None), P("gx", None), P("gx", None),
            P("gx", None, None), P("gx"), P("gx", None), P(), P(), P(), P(),
        ),
        out_specs=P("gx", None),
        check_vma=False,
    )
```

time: 166 us -> 113 us (0.68)
  local copies, waits for them, and re-layouts: 66.2 us -> 5.44 us
  Pallas kernels: 0 us -> 30.2 us
  other arithmetic: 26.1 us -> 1.74 us
  waiting for transfers between devices: 49.1 us -> 54.8 us
  matrix products: 3.41 us -> 0 us
    gather x3 -> x0, local copies, waits for them, and re-layouts: 57.4 us -> none  [the longest x2 51.8 us: pick_rows(): near_picked = table[jnp.clip(near_local, 0, size - 1)]]
    pallas_call x0 -> x1, Pallas kernels: none -> 30.2 us  [finish(): pl.pallas_call(finish_kernel, out_shape=jax.ShapeDtypeStruct((seeds, w_se...]
    concatenate x1, other arithmetic: 11.8 us -> 0.02 us  [on_device(): jnp.concatenate([target_slot.T[:, None, :], jnp.where(live, near, empty_r...]
    reduce_sum x1 -> x0, other arithmetic: 6.33 us -> none  [pick_rows(): neighbour_sum = jnp.sum(near_rows.astype(jnp.float32), axis=2)]
    all_to_all x1, waiting for transfers between devices: 5.77 us -> 10.3 us  [on_device(): lax.all_to_all(served, 'gx', split_axis=0, concat_axis=0, tiled=True)]
    dot_general x3 -> x0, matrix products: 3.41 us -> none  [the longest x1 2.12 us: layers(): jnp.dot(stacked.reshape(seed_rows * targets_here, -1), w_first, preferred...]
    convert_element_type x4 -> x0, other arithmetic: 2.86 us -> none  [the longest x1 1.41 us: layers(): (neighbour_sum / hop2_count[..., None].astype(jnp.float32)).astype(jnp.bf...]
  transfers between devices with their start and end apart: 2 -> 2, of which waited for: 2 -> 2; matrix products, arithmetic and copies ran while one was open for 8% -> 6% of each run, Pallas kernels for 0% -> 0%
where the time goes in v1:
time: 113 us
  waiting for transfers between devices  54.8 us (48%)
  Pallas kernels  30.2 us (27%)
  between operations  13.5 us (12%)
  starting transfers between devices  7.36 us (7%)
  local copies, waits for them, and re-layouts  5.44 us (5%)
  other arithmetic  1.74 us (2%)
    all_gather x1, waiting for transfers between devices, on_device(): hot_all = lax.all_gather(hot_cache, 'gx', axis=0, tiled=True)  43.8 us
    pallas_call x1, Pallas kernels, finish(): pl.pallas_call(finish_kernel, out_shape=jax.ShapeDtypeStruct((seeds, w_se...  30.2 us
    all_to_all x1, waiting for transfers between devices, on_device(): lax.all_to_all(served, 'gx', split_axis=0, concat_axis=0, tiled=True)  10.3 us
    all_to_all x1, starting transfers between devices, on_device(): lax.all_to_all(served, 'gx', split_axis=0, concat_axis=0, tiled=True)  7.32 us
    gather x1, local copies, waits for them, and re-layouts, on_device(): served = cold_table[served_index]  3.2 us
  transfers between devices with their start and end apart: 2, of which 2 were waited for; matrix products, arithmetic and copies ran while one was open for 6% of the time, Pallas kernels for 0%

profile of v1, /device:TPU:0, one launch (start us, length us, event | category | flops | bytes accessed | tf_op | source)
XLA Modules:
  0.0 113.0 jit_solution(10695004589044128312)
XLA Ops:
  6.5 0.0 copy-start
  6.5 0.0 copy-start.6
  6.5 0.0 copy-start.4
  6.5 0.0 copy-start.3
  6.5 0.0 copy-start.5
  6.6 0.0 copy-start.2
  6.6 0.0 all-gather.2.cloned.1.call-start
  6.6 0.7 all-gather.2.cloned.1.call-update
  7.3 0.7 compare_select_fusion
  8.0 0.1 reshape.61
  8.1 0.0 copy-done
  8.1 3.2 %gather_fusion = bf16[1024,128]{1,0:T(8,128)(2,1)S(1)} fusion(bf16[8192,128]{1,0:T(8,128)(2,1)S(1)} %copy-done, s32[1024]{0:T(1024)S(1)} %broadcast_clamp_fusion), kind=kCustom, calls=%fused_computation | custom fusion | bytes 528384 | tf_op jit(solution)/shard_map/gather | solution.py:111
  11.3 0.0 copy-done.6
  11.3 0.1 iota_compare_fusion.1
  11.4 0.9 broadcast_select_fusion
  12.3 7.3 %all-to-all-start = ((bf16[32,32,128]{2,1,0:T(8,128)(2,1)}), bf16[32,32,128]{2,1,0:T(8,128)(2,1)S(1)}, u32[]{:S(2)}, u32[]{:S(2)}) async-start(bf16[32,32,128]{2,1,0:T(8,128)(2,1)} %broadcast_select_fusion), calls=%async_computation | async-start | bytes 524288 | tf_op jit(solution)/shard_map/all_to_all | solution.py:115
  19.7 0.0 copy-done.4
  19.7 0.0 copy-done.3
  19.7 0.7 copy.13.count_two
  20.4 0.0 copy-done.5
  20.4 0.7 copy.14.count_one
  21.2 0.0 copy-done.2
  21.2 0.6 pad.4
  21.8 10.3 %all-to-all-done = bf16[32,32,128]{2,1,0:T(8,128)(2,1)S(1)} async-done(((bf16[32,32,128]{2,1,0:T(8,128)(2,1)}), bf16[32,32,128]{2,1,0:T(8,128)(2,1)S(1)}, u32[]{:S(2)}, u32[]{:S(2)}) %all-to-all-start) | async-done | bytes 262176 | tf_op jit(solution)/shard_map/all_to_all | solution.py:115
  32.1 0.0 copy-start.1
  32.1 43.8 %all-gather.2.cloned.1.call-done.hot = bf16[16384,128]{1,0:T(8,128)(2,1)} async-done(((bf16[512,128]{1,0:T(8,128)(2,1)}), bf16[16384,128]{1,0:T(8,128)(2,1)}) %all-gather.2.cloned.1.call-update) | async-done | bytes 4194320 | tf_op jit(solution)/shard_map/all_gather | solution.py:117
  75.9 0.0 copy-done.1
  75.9 30.2 %finish.1 = f32[128,256]{1,0:T(8,128)} custom-call(s32[24576]{0:T(1024)} %bitcast.17, s32[128]{0:T(128)} %hop1.1, bf16[16384,128]{1,0:T(8,128)(2,1)} %all-gather.2.cloned.1.call-done.hot, bf16[1024,128]{1,0:T(8,128)(2,1)} %bitcast.15, s32[128,11]{1,0:T(8,128)} %copy.13.count_two, s32[128,1]{1,0:T(8,128)} %copy.14.count_one, bf16[256,256]{1,0:T(8,128)(2,1)} %w_first.1, ...), custom_call_target="tpu_custom_call" | custom-call | tf_op jit(solution)/shard_map/finish/pallas_call | solution.py:85
  (4 shorter events, 0.0 us)
Async XLA Ops:
  6.5 1.6 %copy-start = (bf16[8192,128]{1,0:T(8,128)(2,1)S(1)}, bf16[8192,128]{1,0:T(8,128)(2,1)}, u32[]{:S(2)}) copy-start(bf16[8192,128]{1,0:T(8,128)(2,1)} %param.13) | copy-start | bytes 6291460
  6.5 4.8 %copy-start.6 = (s32[1,32]{1,0:T(1,128)S(1)}, s32[1,32]{1,0:T(1,128)}, u32[]{:S(2)}) copy-start(s32[1,32]{1,0:T(1,128)} %param.15) | copy-start | bytes 388
  6.5 13.1 %copy-start.4 = (s32[128,11]{0,1:T(8,128)S(1)}, s32[128,11]{0,1:T(8,128)}, u32[]{:S(2)}) copy-start(s32[128,11]{0,1:T(8,128)} %param.16) | copy-start | bytes 16900
  6.5 13.1 %copy-start.3 = (s32[128,11]{0,1:T(8,128)S(1)}, s32[128,11]{0,1:T(8,128)}, u32[]{:S(2)}) copy-start(s32[128,11]{0,1:T(8,128)} %param.19) | copy-start | bytes 16900
  6.5 13.9 %copy-start.5 = (s32[128]{0:T(128)S(1)}, s32[128]{0:T(128)}, u32[]{:S(2)}) copy-start(s32[128]{0:T(128)} %hop1.1) | copy-start | bytes 1540
  6.6 14.6 %copy-start.2 = (s32[128,11,15]{0,2,1:T(8,128)S(1)}, s32[128,11,15]{0,2,1:T(8,128)}, u32[]{:S(2)}) copy-start(s32[128,11,15]{0,2,1:T(8,128)} %param.17) | copy-start | bytes 253444
  6.6 69.4 %all-gather.2.cloned.1.call-start = ((), (), s32[]{:S(2)}) async-start(), calls=%async_computation.1 | async-start | bytes 4325376 | tf_op jit(solution)/shard_map/all_gather | solution.py:117
  12.3 19.8 %all-to-all-start = ((bf16[32,32,128]{2,1,0:T(8,128)(2,1)}), bf16[32,32,128]{2,1,0:T(8,128)(2,1)S(1)}, u32[]{:S(2)}, u32[]{:S(2)}) async-start(bf16[32,32,128]{2,1,0:T(8,128)(2,1)} %broadcast_select_fusion), calls=%async_computation | async-start | bytes 524288 | tf_op jit(solution)/shard_map/all_to_all | solution.py:115
  32.1 43.8 %copy-start.1 = (bf16[32,32,128]{2,1,0:T(8,128)(2,1)}, bf16[32,32,128]{2,1,0:T(8,128)(2,1)S(1)}, u32[]{:S(2)}) copy-start(bf16[32,32,128]{2,1,0:T(8,128)(2,1)S(1)} %all-to-all-done) | copy-start | bytes 786436
Sparse Core Ops, SparseCore 0:
  10.2 65.6 all-gather.1

commit v2 on v1

v2 whole, which is shorter than its diff:
```python
import functools

import jax
import jax.numpy as jnp
from jax import lax
from jax.experimental import pallas as pl
from jax.experimental.pallas import tpu as pltpu
from jax.sharding import PartitionSpec as P

LANES = 128
HOT_REQ = 64
TASKS = 4

VMEM = pl.BlockSpec(memory_space=pltpu.VMEM)
SMEM = pl.BlockSpec(memory_space=pltpu.SMEM)


def split(size):
    bits = size.bit_length() - 1
    assert size == 1 << bits
    return bits


def one_hot(index, size):
    iota = lax.broadcasted_iota(jnp.int32, (size, index.shape[1]), 0)
    return jnp.where(iota == index, 1.0, 0.0).astype(jnp.bfloat16)


def rank_kernel(own, near, rank):
    owners, lines = rank.shape[0], rank.shape[1]
    high = owners * lines
    bits = split(LANES)
    counts = jnp.zeros((high, LANES), jnp.float32)
    for t in range(own.shape[0]):
        rows = [own[t : t + 1, :]] + [near[t, k : k + 1, :] for k in range(near.shape[1])]
        outer = jnp.concatenate([one_hot(r >> bits, high) for r in rows], 1)
        inner = jnp.concatenate([one_hot(r & (LANES - 1), LANES) for r in rows], 1)
        counts += lax.dot_general(
            outer, inner, (((1,), (1,)), ((), ())), preferred_element_type=jnp.float32
        )
    used = counts > 0.0
    flags = jnp.where(used, 1.0, 0.0).astype(jnp.bfloat16)
    a = lax.broadcasted_iota(jnp.int32, (LANES, LANES), 0)
    b = lax.broadcasted_iota(jnp.int32, (LANES, LANES), 1)
    before = jnp.where(a < b, 1.0, 0.0).astype(jnp.bfloat16)
    inside = jnp.dot(flags, before, preferred_element_type=jnp.float32)
    every = jnp.ones((LANES, LANES), jnp.bfloat16)
    sums = jnp.dot(flags, every, preferred_element_type=jnp.float32).astype(jnp.bfloat16)
    a = lax.broadcasted_iota(jnp.int32, (high, high), 0)
    b = lax.broadcasted_iota(jnp.int32, (high, high), 1)
    line_bits = split(lines)
    earlier = (a > b) & ((a >> line_bits) == (b >> line_bits))
    earlier = jnp.where(earlier, 1.0, 0.0).astype(jnp.bfloat16)
    offset = jnp.dot(earlier, sums, preferred_element_type=jnp.float32)
    value = jnp.where(used, inside + offset, -1.0)
    rank[...] = value.reshape(rank.shape)


def select_kernel(group, asked, hot, cold, out):
    owners, lines = asked.shape[0], asked.shape[1]
    cold_rows = cold.shape[1]
    want = lax.broadcasted_iota(jnp.int32, (HOT_REQ, LANES), 0).astype(jnp.float32)

    def some(i, carry):
        picks = []
        for g in range(group):
            row = asked[i * group + g]
            picks.append(
                jnp.concatenate(
                    [jnp.where(want == row[r : r + 1, :], 1.0, 0.0) for r in range(lines)], 1
                ).astype(jnp.bfloat16)
            )
        picked = jnp.dot(
            jnp.concatenate(picks, 0), hot[...], preferred_element_type=jnp.float32
        ).astype(out.dtype)
        for g in range(group):
            d = i * group + g
            out[d, pl.ds(0, HOT_REQ), :] = picked[g * HOT_REQ : (g + 1) * HOT_REQ]
            out[d, pl.ds(HOT_REQ, cold_rows), :] = cold[d]
        return carry

    lax.fori_loop(0, owners // group, some, 0)


def remap_kernel(cold_rows, own, near, count, rank, out):
    owners, lines = rank.shape[0], rank.shape[1]
    high = owners * lines
    targets, fan = near.shape[0], near.shape[1]
    stride = out.shape[0] // (fan + 1)
    bits, line_bits, cold_bits = split(LANES), split(lines), split(cold_rows)
    per = HOT_REQ + cold_rows
    first_cold = high * LANES
    by_low = jnp.transpose(rank[...].reshape(high, LANES)).astype(jnp.bfloat16)
    low = lax.broadcasted_iota(jnp.int32, (LANES, LANES), 0)
    empty = jnp.full((1, LANES), owners * per, jnp.int32)
    for t in range(targets):
        rows = [own[t : t + 1, :]] + [near[t, k : k + 1, :] for k in range(fan)]
        outer = jnp.concatenate([one_hot(r >> bits, high) for r in rows], 1)
        found = jnp.dot(by_low, outer, preferred_element_type=jnp.float32)
        for k, r in enumerate(rows):
            mine = jnp.where(
                low == (r & (LANES - 1)), found[:, k * LANES : (k + 1) * LANES], 0.0
            )
            rank_here = jnp.sum(mine, 0, keepdims=True).astype(jnp.int32)
            as_hot = (r >> (bits + line_bits)) * per + rank_here
            c = r - first_cold
            as_cold = (c >> cold_bits) * per + HOT_REQ + (c & (cold_rows - 1))
            row = jnp.where(c >= 0, as_cold, as_hot)
            if k > 0:
                row = jnp.where(count[t : t + 1, :] > k - 1, row, empty)
            out[k * stride + t : k * stride + t + 1, :] = row
    for k in range(fan + 1):
        for t in range(targets, stride):
            out[k * stride + t : k * stride + t + 1, :] = empty


def plan_kernel(half, hop1, count, first, second, sizes):
    targets, seeds = count.shape

    def one_seed(s, carry):
        a, b = carry
        n = hop1[s]
        for t in range(targets):
            live = t <= n
            more = live & (count[t, s] > half - 1)
            first[a] = t * seeds + s
            second[b] = t * seeds + s
            a += live.astype(jnp.int32)
            b += more.astype(jnp.int32)
        return a, b

    a, b = lax.fori_loop(0, seeds, one_seed, (jnp.int32(0), jnp.int32(0)))
    for i in range(TASKS):
        first[a + i] = targets * seeds
        second[b + i] = targets * seeds
    sizes[0] = (a + TASKS - 1) // TASKS
    sizes[1] = (b + TASKS - 1) // TASKS


def tree(rows):
    while len(rows) > 1:
        rows = [a + b for a, b in zip(rows[::2], rows[1::2])] + (
            [rows[-1]] if len(rows) % 2 else []
        )
    return rows[0]


def finish_kernel(
    half, slots, first, second, sizes, rows, count_two, count_one,
    w_first, b_first, w_second, b_second, out, table, own, total,
):
    n_rows, width = rows.shape
    seeds, targets = count_two.shape
    step = own.shape[0]
    per = slots.shape[0] // step
    table[pl.ds(0, n_rows), :] = rows[...].astype(jnp.float32)
    table[pl.ds(n_rows, 8), :] = jnp.zeros((8, width), jnp.float32)

    def pick(k, code):
        return table[pl.ds(slots[code + k * step], 1), :]

    def first_part(i, carry):
        for g in range(TASKS):
            code = first[i * TASKS + g]
            own[pl.ds(code, 1), :] = pick(0, code)
            total[pl.ds(code, 1), :] = tree([pick(k, code) for k in range(1, half)])
        return carry

    def second_part(i, carry):
        codes = [second[i * TASKS + g] for g in range(TASKS)]
        held = [total[pl.ds(code, 1), :] for code in codes]
        sums = [
            h + tree([pick(k, code) for k in range(half, per)]) for h, code in zip(held, codes)
        ]
        for code, value in zip(codes, sums):
            total[pl.ds(code, 1), :] = value
        return carry

    lax.fori_loop(0, sizes[0], first_part, 0)
    lax.fori_loop(0, sizes[1], second_part, 0)

    pooled = jnp.zeros((seeds, w_first.shape[1]), jnp.float32)
    near = count_one[...]
    for t in range(targets):
        here = pl.ds(t * seeds, seeds)
        aggregate = total[here, :] / count_two[:, t : t + 1].astype(jnp.float32)
        stacked = jnp.concatenate(
            [own[here, :].astype(jnp.bfloat16), aggregate.astype(jnp.bfloat16)], -1
        )
        hidden = jnp.dot(stacked, w_first[...], preferred_element_type=jnp.float32) + b_first[...]
        hidden = jnp.maximum(hidden, 0.0).astype(jnp.bfloat16)
        if t == 0:
            seed_hidden = hidden
        else:
            pooled += jnp.where(near > t - 1, hidden.astype(jnp.float32), 0.0)
    pooled = (pooled / near.astype(jnp.float32)).astype(jnp.bfloat16)
    joined = jnp.concatenate([seed_hidden, pooled], -1)
    out[...] = jnp.dot(joined, w_second[...], preferred_element_type=jnp.float32) + b_second[...]


def on_device(
    hot_cache, cold_table, serve_index, serve_count, target_slot, hop2_slot,
    hop1_count, hop2_count, w_first, b_first, w_second, b_second,
):
    owners, cold_rows = serve_index.shape[1:]
    hot_dev, width = hot_cache.shape
    lines = hot_dev // LANES
    seeds, targets, fan = hop2_slot.shape
    half = (fan + 1) // 2
    step = (targets + 1) * seeds
    own_slot = target_slot.T
    near_slot = jnp.transpose(hop2_slot, (1, 2, 0))
    count_t = hop2_count.T

    rank = pl.pallas_call(
        rank_kernel,
        out_shape=jax.ShapeDtypeStruct((owners, lines, LANES), jnp.float32),
        in_specs=[VMEM, VMEM],
        out_specs=VMEM,
        name="rank",
    )(own_slot, near_slot)
    asked = lax.all_to_all(rank, "gx", split_axis=0, concat_axis=0, tiled=True)

    served_index = serve_index[0]
    slot_iota = lax.broadcasted_iota(jnp.int32, served_index.shape, 1)
    served = cold_table[served_index]
    served = jnp.where(
        (slot_iota < serve_count[0][:, None])[..., None], served, jnp.zeros((), cold_table.dtype)
    )
    answer = pl.pallas_call(
        functools.partial(select_kernel, 8 if owners % 8 == 0 else 1),
        out_shape=jax.ShapeDtypeStruct((owners, HOT_REQ + cold_rows, width), hot_cache.dtype),
        in_specs=[VMEM] * 3,
        out_specs=VMEM,
        name="select",
    )(asked, hot_cache, served)
    received = lax.all_to_all(answer, "gx", split_axis=0, concat_axis=0, tiled=True)

    slots = pl.pallas_call(
        functools.partial(remap_kernel, cold_rows),
        out_shape=jax.ShapeDtypeStruct(((fan + 1) * (targets + 1), seeds), jnp.int32),
        in_specs=[VMEM] * 4,
        out_specs=VMEM,
        name="remap",
    )(own_slot, near_slot, count_t, rank)
    first, second, sizes = pl.pallas_call(
        functools.partial(plan_kernel, half),
        out_shape=(
            jax.ShapeDtypeStruct((step,), jnp.int32),
            jax.ShapeDtypeStruct((step,), jnp.int32),
            jax.ShapeDtypeStruct((2,), jnp.int32),
        ),
        in_specs=[SMEM, SMEM],
        out_specs=(SMEM, SMEM, SMEM),
        name="plan",
    )(hop1_count, count_t)

    rows = owners * (HOT_REQ + cold_rows)
    return pl.pallas_call(
        functools.partial(finish_kernel, half),
        out_shape=jax.ShapeDtypeStruct((seeds, w_second.shape[1]), jnp.float32),
        in_specs=[SMEM] * 4 + [VMEM] * 7,
        out_specs=VMEM,
        scratch_shapes=[
            pltpu.VMEM((rows + 8, width), jnp.float32),
            pltpu.VMEM((step, width), jnp.float32),
            pltpu.VMEM((step, width), jnp.float32),
        ],
        name="finish",
    )(
        slots.reshape(-1), first, second, sizes, received.reshape(rows, width),
        hop2_count, hop1_count[:, None], w_first, b_first[None], w_second, b_second[None],
    )


def solution(mesh):
    return jax.shard_map(
        on_device,
        mesh=mesh,
        in_specs=(
            P("gx", None), P("gx", None), P("gx", None, None), P("gx", None), P("gx", None),
            P("gx", None, None), P("gx"), P("gx", None), P(), P(), P(), P(),
        ),
        out_specs=P("gx", None),
        check_vma=False,
    )
```

time: 113 us -> 63.4 us (0.56)
  waiting for transfers between devices: 54.8 us -> 7.12 us
  between operations: 13.5 us -> 0.07 us
  Pallas kernels: 30.2 us -> 35.4 us
  starting transfers between devices: 7.36 us -> 11.4 us
    all_gather x1 -> x0, waiting for transfers between devices: 43.8 us -> none  [on_device(): hot_all = lax.all_gather(hot_cache, 'gx', axis=0, tiled=True)]
    pallas_call x1 -> x5, Pallas kernels: 30.2 us -> 35.4 us  [the longest x1 14.8 us: on_device(): pl.pallas_call(functools.partial(finish_kernel, half), out_shape=jax.Shap...]
    all_to_all x1 -> x2, starting transfers between devices: 7.32 us -> 11.4 us  [the longest x1 7.33 us: on_device(): asked = lax.all_to_all(rank, 'gx', split_axis=0, concat_axis=0, tiled=True)]
    all_to_all x1 -> x2, waiting for transfers between devices: 10.3 us -> 7.12 us  [the longest x1 5.38 us: on_device(): lax.all_to_all(answer, 'gx', split_axis=0, concat_axis=0, tiled=True)]
    unnamed x15 -> x11, local copies, waits for them, and re-layouts: 0.78 us -> 2.24 us
  transfers between devices with their start and end apart: 2 -> 2, of which waited for: 2 -> 2; matrix products, arithmetic and copies ran while one was open for 6% -> 11% of each run, Pallas kernels for 0% -> 22%
where the time goes in v2:
time: 63.4 us; the launch traced here: 62.6 us
  Pallas kernels  35.4 us (56%)
  starting transfers between devices  11.4 us (18%)
  waiting for transfers between devices  7.12 us (11%)
  local copies, waits for them, and re-layouts  6.25 us (10%)
  other arithmetic  2.36 us (4%)
    pallas_call x1, Pallas kernels, on_device(): pl.pallas_call(functools.partial(finish_kernel, half), out_shape=jax.Shap...  14.8 us
    pallas_call x1, Pallas kernels, on_device(): pl.pallas_call(functools.partial(plan_kernel, half), out_shape=(jax.Shape...  8.32 us
    all_to_all x1, starting transfers between devices, on_device(): asked = lax.all_to_all(rank, 'gx', split_axis=0, concat_axis=0, tiled=True)  7.33 us
    pallas_call x1, Pallas kernels, on_device(): pl.pallas_call(functools.partial(remap_kernel, cold_rows), out_shape=jax....  5.4 us
    all_to_all x1, waiting for transfers between devices, on_device(): lax.all_to_all(answer, 'gx', split_axis=0, concat_axis=0, tiled=True)  5.38 us
    all_to_all x1, starting transfers between devices, on_device(): lax.all_to_all(answer, 'gx', split_axis=0, concat_axis=0, tiled=True)  4.11 us
    pallas_call x1, Pallas kernels, on_device(): pl.pallas_call(rank_kernel, out_shape=jax.ShapeDtypeStruct((owners, lines...  3.76 us
    gather x1, local copies, waits for them, and re-layouts, on_device(): served = cold_table[served_index]  3.2 us
  transfers between devices with their start and end apart: 2, of which 2 were waited for; matrix products, arithmetic and copies ran while one was open for 11% of the time, Pallas kernels for 22%

profile of v2, /device:TPU:0, one launch (start us, length us, event | category | flops | bytes accessed | tf_op | source)
XLA Modules:
  0.0 62.6 jit_solution(3700670648515893252)
XLA Ops:
  0.0 0.0 copy-start
  0.0 3.8 %rank.1 = f32[32,4,128]{2,1,0:T(4,128)} custom-call(s32[11,128]{1,0:T(8,128)} %bitcast.21, s32[11,15,128]{2,1,0:T(8,128)} %bitcast.17), custom_call_target="tpu_custom_call" | custom-call | tf_op jit(solution)/shard_map/rank/pallas_call | solution.py:215
  3.8 7.3 %all-to-all-start = ((f32[32,4,128]{2,1,0:T(4,128)}), f32[32,4,128]{2,1,0:T(4,128)S(1)}, u32[]{:S(2)}, u32[]{:S(2)}) async-start(f32[32,4,128]{2,1,0:T(4,128)} %rank.1), calls=%async_computation | async-start | bytes 131072 | tf_op jit(solution)/shard_map/all_to_all | solution.py:222
  11.1 0.7 %compare_select_fusion = s32[32,32,1]{1,0,2:T(8,128)S(1)} fusion(s32[1,32,32]{2,1,0:T(8,128)} %param.14), kind=kLoop, calls=%fused_computation.2 | loop fusion | flops 3072 | bytes 8192 | tf_op jit(solution)/shard_map/select_n | solution.py:226
  11.8 0.1 reshape.60
  11.9 0.7 %iota_compare_fusion = pred[32,32]{1,0:T(8,128)(4,1)S(1)} fusion(s32[32]{0:T(128)} %bitcast.26), kind=kLoop, calls=%fused_computation.3 | loop fusion | flops 1024 | bytes 1152 | tf_op jit(solution)/shard_map/lt | solution.py:228
  12.6 0.0 copy-done
  12.6 3.2 %gather_fusion = bf16[1024,128]{1,0:T(8,128)(2,1)S(1)} fusion(bf16[8192,128]{1,0:T(8,128)(2,1)S(1)} %copy-done, s32[1024]{0:T(1024)S(1)} %broadcast_clamp_fusion), kind=kCustom, calls=%fused_computation | custom fusion | bytes 528384 | tf_op jit(solution)/shard_map/gather | solution.py:226
  15.8 0.0 copy-start.3
  15.9 0.0 copy-start.4
  15.9 0.9 %broadcast_select_fusion.cold = bf16[32,32,128]{2,1,0:T(8,128)(2,1)} fusion(bf16[32,32,128]{2,1,0:T(8,128)(2,1)S(1)} %bitcast.15, pred[32,32]{1,0:T(8,128)(4,1)S(1)} %iota_compare_fusion), kind=kLoop, calls=%fused_computation.1 | loop fusion | flops 131072 | bytes 525312 | tf_op jit(solution)/shard_map/jit(_where)/select_n | solution.py:227
  16.8 1.7 %all-to-all-done.asked = f32[32,4,128]{2,1,0:T(4,128)S(1)} async-done(((f32[32,4,128]{2,1,0:T(4,128)}), f32[32,4,128]{2,1,0:T(4,128)S(1)}, u32[]{:S(2)}, u32[]{:S(2)}) %all-to-all-start) | async-done | bytes 65568 | tf_op jit(solution)/shard_map/all_to_all | solution.py:222
  18.5 0.0 copy-start.2
  18.5 0.6 copy-done.2
  19.1 3.1 %select.1 = bf16[32,96,128]{2,1,0:T(8,128)(2,1)} custom-call(f32[32,4,128]{2,1,0:T(4,128)} %copy-done.2, bf16[512,128]{1,0:T(8,128)(2,1)} %hot.1, bf16[32,32,128]{2,1,0:T(8,128)(2,1)} %broadcast_select_fusion.cold), custom_call_target="tpu_custom_call" | custom-call | tf_op jit(solution)/shard_map/select/pallas_call | solution.py:230
  22.3 4.1 %all-to-all-start.1 = ((bf16[32,96,128]{2,1,0:T(8,128)(2,1)}), bf16[32,96,128]{2,1,0:T(8,128)(2,1)S(1)}, u32[]{:S(2)}, u32[]{:S(2)}) async-start(bf16[32,96,128]{2,1,0:T(8,128)(2,1)} %select.1), calls=%async_computation.1 | async-start | bytes 1572864 | tf_op jit(solution)/shard_map/all_to_all | solution.py:237
  26.4 0.0 copy-done.3
  26.4 0.7 %copy.13.count_two = s32[128,11]{1,0:T(8,128)} copy(s32[128,11]{0,1:T(8,128)S(1)} %copy-done.3) | data formatting | bytes 11264 | tf_op args[7]
  27.1 5.4 %remap.1 = s32[192,128]{1,0:T(8,128)} custom-call(s32[11,128]{1,0:T(8,128)} %bitcast.22, s32[11,15,128]{2,1,0:T(8,128)} %bitcast.18, s32[11,128]{1,0:T(8,128)} %bitcast.19, f32[32,4,128]{2,1,0:T(4,128)} %rank.1), custom_call_target="tpu_custom_call" | custom-call | tf_op jit(solution)/shard_map/remap/pallas_call | solution.py:239
  32.5 8.3 %plan.1 = (s32[1536]{0:T(1024)}, s32[1536]{0:T(1024)}, s32[2]{0:T(128)}) custom-call(s32[128]{0:T(128)} %hop1.1, s32[11,128]{1,0:T(8,128)} %bitcast.20), custom_call_target="tpu_custom_call" | custom-call | tf_op jit(solution)/shard_map/plan/pallas_call | solution.py:246
  40.8 0.0 copy-done.4
  40.9 0.7 %copy.14.count_one = s32[128,1]{1,0:T(8,128)} copy(s32[128,1]{0,1:T(1,128)S(1)} %bitcast.23) | data formatting | bytes 1024 | tf_op jit(solution)/shard_map/broadcast_in_dim | solution.py:272
  41.6 5.4 %all-to-all-done.1 = bf16[32,96,128]{2,1,0:T(8,128)(2,1)S(1)} async-done(((bf16[32,96,128]{2,1,0:T(8,128)(2,1)}), bf16[32,96,128]{2,1,0:T(8,128)(2,1)S(1)}, u32[]{:S(2)}, u32[]{:S(2)}) %all-to-all-start.1) | async-done | bytes 786464 | tf_op jit(solution)/shard_map/all_to_all | solution.py:237
  47.0 0.0 copy-start.1
  47.0 0.9 %copy-done.1 = bf16[32,96,128]{2,1,0:T(8,128)(2,1)} copy-done((bf16[32,96,128]{2,1,0:T(8,128)(2,1)}, bf16[32,96,128]{2,1,0:T(8,128)(2,1)S(1)}, u32[]{:S(2)}) %copy-start.1) | copy-done | bytes 786456
  47.8 14.8 %finish.1 = f32[128,256]{1,0:T(8,128)} custom-call(s32[24576]{0:T(1024)} %bitcast.16, s32[1536]{0:T(1024)} %get-tuple-element.8.first, s32[1536]{0:T(1024)} %get-tuple-element.9.second, s32[2]{0:T(128)} %get-tuple-element.10.sizes, bf16[3072,128]{1,0:T(8,128)(2,1)} %bitcast.14, s32[128,11]{1,0:T(8,128)} %copy.13.count_two, s32[128,1]{1,0:T(8,128)} %copy.14.count_one, ...), custom_call_target="tpu_custom_call" | custom-call | tf_op jit(solution)/shard_map/finish/pallas_call | solution.py:259
  (1 shorter events, 0.0 us)
Async XLA Ops:
  0.0 12.6 %copy-start = (bf16[8192,128]{1,0:T(8,128)(2,1)S(1)}, bf16[8192,128]{1,0:T(8,128)(2,1)}, u32[]{:S(2)}) copy-start(bf16[8192,128]{1,0:T(8,128)(2,1)} %param.13) | copy-start | bytes 6291460
  3.8 14.7 %all-to-all-start = ((f32[32,4,128]{2,1,0:T(4,128)}), f32[32,4,128]{2,1,0:T(4,128)S(1)}, u32[]{:S(2)}, u32[]{:S(2)}) async-start(f32[32,4,128]{2,1,0:T(4,128)} %rank.1), calls=%async_computation | async-start | bytes 131072 | tf_op jit(solution)/shard_map/all_to_all | solution.py:222
  15.8 10.5 %copy-start.3 = (s32[128,11]{0,1:T(8,128)S(1)}, s32[128,11]{0,1:T(8,128)}, u32[]{:S(2)}) copy-start(s32[128,11]{0,1:T(8,128)} %param.19) | copy-start | bytes 16900
  15.9 25.0 %copy-start.4 = (s32[128]{0:T(128)S(1)}, s32[128]{0:T(128)}, u32[]{:S(2)}) copy-start(s32[128]{0:T(128)} %hop1.1) | copy-start | bytes 1540
  18.5 0.6 copy-start.2
  22.3 24.7 %all-to-all-start.1 = ((bf16[32,96,128]{2,1,0:T(8,128)(2,1)}), bf16[32,96,128]{2,1,0:T(8,128)(2,1)S(1)}, u32[]{:S(2)}, u32[]{:S(2)}) async-start(bf16[32,96,128]{2,1,0:T(8,128)(2,1)} %select.1), calls=%async_computation.1 | async-start | bytes 1572864 | tf_op jit(solution)/shard_map/all_to_all | solution.py:237
  47.0 0.9 %copy-start.1 = (bf16[32,96,128]{2,1,0:T(8,128)(2,1)}, bf16[32,96,128]{2,1,0:T(8,128)(2,1)S(1)}, u32[]{:S(2)}) copy-start(bf16[32,96,128]{2,1,0:T(8,128)(2,1)S(1)} %all-to-all-done.1) | copy-start | bytes 2359300

commit v3 on v2

v3 whole, which is shorter than its diff:
```python
import functools

import jax
import jax.numpy as jnp
from jax import lax
from jax.experimental import pallas as pl
from jax.experimental.pallas import tpu as pltpu
from jax.sharding import PartitionSpec as P


LANES = 128
HOT_REQ = 64
PEERS = 8
TASKS = 8

VMEM = pl.BlockSpec(memory_space=pltpu.VMEM)
SMEM = pl.BlockSpec(memory_space=pltpu.SMEM)
ANY = pl.BlockSpec(memory_space=pl.ANY)


def in_vmem(x):
    return pltpu.with_memory_space_constraint(x, pltpu.VMEM)


def split(size):
    bits = size.bit_length() - 1
    assert size == 1 << bits
    return bits


def one_hot(index, size):
    iota = lax.broadcasted_iota(jnp.int32, (size, index.shape[1]), 0)
    return jnp.where(iota == index, 1.0, 0.0).astype(jnp.bfloat16)


def rank_kernel(own, near, rank, ask, held):
    peers, groups = ask.shape[0], held.shape[0] // ask.shape[0]
    high = rank.shape[0]
    lines = high // held.shape[0]
    bits = split(LANES)
    counts = jnp.zeros((high, LANES), jnp.float32)
    for t in range(own.shape[0]):
        rows = [own[t : t + 1, :]] + [near[t, k : k + 1, :] for k in range(near.shape[1])]
        outer = jnp.concatenate([one_hot(r >> bits, high) for r in rows], 1)
        inner = jnp.concatenate([one_hot(r & (LANES - 1), LANES) for r in rows], 1)
        counts += lax.dot_general(
            outer, inner, (((1,), (1,)), ((), ())), preferred_element_type=jnp.float32
        )
    used = counts > 0.0
    flags = jnp.where(used, 1.0, 0.0).astype(jnp.bfloat16)
    a = lax.broadcasted_iota(jnp.int32, (LANES, LANES), 0)
    b = lax.broadcasted_iota(jnp.int32, (LANES, LANES), 1)
    before = jnp.where(a < b, 1.0, 0.0).astype(jnp.bfloat16)
    inside = jnp.dot(flags, before, preferred_element_type=jnp.float32)
    every = jnp.ones((LANES, LANES), jnp.bfloat16)
    sums = jnp.dot(flags, every, preferred_element_type=jnp.float32).astype(jnp.bfloat16)
    a = lax.broadcasted_iota(jnp.int32, (high, high), 0)
    b = lax.broadcasted_iota(jnp.int32, (high, high), 1)
    line_bits = split(lines)
    earlier = (a > b) & ((a >> line_bits) == (b >> line_bits))
    earlier = jnp.where(earlier, 1.0, 0.0).astype(jnp.bfloat16)
    offset = jnp.dot(earlier, sums, preferred_element_type=jnp.float32)
    value = jnp.where(used, inside + offset, -1.0)
    rank[...] = value
    held[...] = value.reshape(held.shape)
    here = lax.axis_index("gx") // peers
    for p in range(peers):
        ask[p] = jnp.concatenate([held[(here ^ g) * peers + p] for g in range(groups)], 0)


def pack_kernel(wanted, live, table, hot, *refs):
    (wide, raw, stage, sems), outs = refs[-4:], refs[:-4]
    n_hot, cold_rows = hot.shape[0], stage.shape[0]
    pieces = sems.shape[0]
    size = table.shape[0] // pieces
    copies = [
        pltpu.make_async_copy(
            table.at[pl.ds(i * size, size)], raw.at[pl.ds(i * size, size)], sems.at[i]
        )
        for i in range(pieces)
    ]
    for copy in copies:
        copy.start()
    for out in outs[1:]:
        out[pl.ds(0, n_hot), :] = hot[...]
    for i, copy in enumerate(copies):
        copy.wait()
        here = pl.ds(i * size, size)
        wide[here, :] = raw[here, :].astype(jnp.float32)
    peers = outs[0].shape[0] // cold_rows
    group = lax.axis_index("gx") // peers
    line = lax.broadcasted_iota(jnp.int32, stage.shape, 0)
    for g, out in enumerate(outs):
        base = out.shape[0] - peers * cold_rows

        def one_device(p, carry, g=g, out=out, base=base):
            d = (group ^ g) * peers + p
            for j in range(cold_rows):
                stage[j : j + 1, :] = wide[pl.ds(wanted[0, d, j], 1), :]
            kept = jnp.where(line < live[0, d], stage[...], 0.0).astype(out.dtype)
            out[pl.ds(pl.multiple_of(base + p * cold_rows, cold_rows), cold_rows), :] = kept
            return carry

        lax.fori_loop(0, peers, one_device, 0)


def select_kernel(asked, hot, *refs):
    packs, out = refs[:-1], refs[-1]
    peers = asked.shape[0]
    n_hot, groups = hot.shape[0], len(packs)
    lines = n_hot // LANES
    cold_rows = packs[0].shape[0] // peers
    want = lax.broadcasted_iota(jnp.int32, (HOT_REQ, LANES), 0).astype(jnp.float32)
    for g, pack in enumerate(packs):
        shard = hot[...] if g == 0 else pack[0:n_hot, :]
        first = pack.shape[0] - peers * cold_rows
        picks = []
        for p in range(peers):
            rows = [asked[p, g * lines + r : g * lines + r + 1, :] for r in range(lines)]
            picks.append(
                jnp.concatenate([jnp.where(want == row, 1.0, 0.0) for row in rows], 1).astype(
                    jnp.bfloat16
                )
            )
        picked = jnp.dot(
            jnp.concatenate(picks, 0), shard, preferred_element_type=jnp.float32
        ).astype(out.dtype)
        for p in range(peers):
            out[p, g * HOT_REQ : (g + 1) * HOT_REQ, :] = picked[p * HOT_REQ : (p + 1) * HOT_REQ]
            place = groups * HOT_REQ + g * cold_rows
            out[p, place : place + cold_rows, :] = pack[
                first + p * cold_rows : first + (p + 1) * cold_rows, :
            ]


def remap_kernel(peers, owners, cold_rows, half, own, near, count, ones, rank, out, place):
    high = rank.shape[0]
    targets, fan = near.shape[0], near.shape[1]
    stride = out.shape[0] // (fan + 1)
    bits, peer_bits = split(LANES), split(peers)
    owner_bits = split(high * LANES // owners)
    groups = owners // peers
    first_cold = high * LANES
    here = lax.axis_index("gx") // peers
    by_low = jnp.transpose(rank[...]).astype(jnp.bfloat16)
    low = lax.broadcasted_iota(jnp.int32, (LANES, LANES), 0)
    per = HOT_REQ + cold_rows
    cold_bits = split(cold_rows)
    empty = jnp.full((1, LANES), owners * per, jnp.int32)
    for t in range(targets):
        rows = [own[t : t + 1, :]] + [near[t, k : k + 1, :] for k in range(fan)]
        outer = jnp.concatenate([one_hot(r >> bits, high) for r in rows], 1)
        found = jnp.dot(by_low, outer, preferred_element_type=jnp.float32)
        for k, r in enumerate(rows):
            mine = jnp.where(
                low == (r & (LANES - 1)), found[:, k * LANES : (k + 1) * LANES], 0.0
            )
            rank_here = jnp.sum(mine, 0, keepdims=True).astype(jnp.int32)
            as_cold = r - first_cold
            is_cold = as_cold >= 0
            owner = jnp.where(is_cold, as_cold >> cold_bits, r >> owner_bits)
            group = (owner >> peer_bits) ^ here
            inside = jnp.where(
                is_cold,
                groups * HOT_REQ + group * cold_rows + (as_cold & (cold_rows - 1)),
                group * HOT_REQ + rank_here,
            )
            row = (owner & (peers - 1)) * (groups * per) + inside
            if k > 0:
                row = jnp.where(count[t : t + 1, :] > k - 1, row, empty)
            out[k * stride + t : k * stride + t + 1, :] = row
    for k in range(fan + 1):
        for t in range(targets, stride):
            out[k * stride + t : k * stride + t + 1, :] = empty
    node = lax.broadcasted_iota(jnp.int32, count.shape, 0)
    more = jnp.where((count[...] > half - 1) & (node <= ones[...]), 1.0, 0.0)
    a = lax.broadcasted_iota(jnp.int32, (LANES, LANES), 0)
    b = lax.broadcasted_iota(jnp.int32, (LANES, LANES), 1)
    before = jnp.where(a < b, 1.0, 0.0).astype(jnp.bfloat16)
    column = jnp.broadcast_to(jnp.sum(more, 0, keepdims=True), count.shape).astype(jnp.bfloat16)
    spot = jnp.dot(column, before, preferred_element_type=jnp.float32)
    spots, upper = [], jnp.zeros((1, LANES), jnp.float32)
    for t in range(targets):
        spots.append(spot[t : t + 1, :] + upper)
        upper = upper + more[t : t + 1, :]
    place[...] = jnp.concatenate(spots, 0).astype(jnp.int32)


def plan_kernel(hop1, place, first, second, sizes):
    seeds = hop1.shape[0]
    targets = place.shape[0] // seeds
    parts = [place.at[pl.ds(t * seeds, seeds)] for t in range(targets)]

    def one_seed(s, a):
        for t in range(targets):
            first[a + t] = t * seeds + s
        for t in range(targets):
            second[parts[t][s]] = t * seeds + s
        return a + hop1[s] + 1

    a = lax.fori_loop(0, seeds, one_seed, jnp.int32(0))
    last = targets * seeds - 1
    b = place[last] + 1
    for i in range(TASKS):
        first[a + i] = targets * seeds
        second[b + i] = targets * seeds
    sizes[0] = (a + TASKS - 1) // TASKS
    sizes[1] = (b + TASKS - 1) // TASKS


def tree(rows):
    while len(rows) > 1:
        rows = [a + b for a, b in zip(rows[::2], rows[1::2])] + (
            [rows[-1]] if len(rows) % 2 else []
        )
    return rows[0]


def finish_kernel(
    half, slots_in, first, second, sizes, rows, count_two, count_one,
    w_first_in, b_first, w_second_in, b_second, out,
    table, own, total, slots, w_first, w_second, sems,
):
    n_rows, width = rows.shape
    seeds, targets = count_two.shape
    step = own.shape[0]
    per = slots.shape[0] // step
    copies = [
        pltpu.make_async_copy(slots_in.at[here], slots.at[here], sems.at[i])
        for i, here in enumerate((pl.ds(0, half * step), pl.ds(half * step, (per - half) * step)))
    ]
    copies.append(pltpu.make_async_copy(w_first_in, w_first, sems.at[2]))
    copies.append(pltpu.make_async_copy(w_second_in, w_second, sems.at[3]))
    for copy in copies:
        copy.start()
    table[pl.ds(0, n_rows), :] = rows[...].astype(jnp.float32)
    table[pl.ds(n_rows, 8), :] = jnp.zeros((8, width), jnp.float32)
    copies[0].wait()

    parts = [slots.at[pl.ds(k * step, step)] for k in range(per)]

    def pick(k, code):
        return table[pl.ds(parts[k][code], 1), :]

    def first_part(i, carry):
        for g in range(TASKS):
            code = first[i * TASKS + g]
            own[pl.ds(code, 1), :] = pick(0, code)
            total[pl.ds(code, 1), :] = tree([pick(k, code) for k in range(1, half)])
        return carry

    def second_part(i, carry):
        codes = [second[i * TASKS + g] for g in range(TASKS)]
        held = [total[pl.ds(code, 1), :] for code in codes]
        sums = [
            h + tree([pick(k, code) for k in range(half, per)]) for h, code in zip(held, codes)
        ]
        for code, value in zip(codes, sums):
            total[pl.ds(code, 1), :] = value
        return carry

    lax.fori_loop(0, sizes[0], first_part, 0)
    copies[1].wait()
    lax.fori_loop(0, sizes[1], second_part, 0)
    copies[2].wait()
    copies[3].wait()

    pooled = jnp.zeros((seeds, w_first.shape[1]), jnp.float32)
    near = count_one[...]
    for t in range(targets):
        here = pl.ds(t * seeds, seeds)
        aggregate = total[here, :] / count_two[:, t : t + 1].astype(jnp.float32)
        stacked = jnp.concatenate(
            [own[here, :].astype(jnp.bfloat16), aggregate.astype(jnp.bfloat16)], -1
        )
        hidden = jnp.dot(stacked, w_first[...], preferred_element_type=jnp.float32) + b_first[...]
        hidden = jnp.maximum(hidden, 0.0).astype(jnp.bfloat16)
        if t == 0:
            seed_hidden = hidden
        else:
            pooled += jnp.where(near > t - 1, hidden.astype(jnp.float32), 0.0)
    pooled = (pooled / near.astype(jnp.float32)).astype(jnp.bfloat16)
    joined = jnp.concatenate([seed_hidden, pooled], -1)
    out[...] = jnp.dot(joined, w_second[...], preferred_element_type=jnp.float32) + b_second[...]


def forward(
    hot_cache, cold_table, serve_index, serve_count, target_slot, hop2_slot,
    hop1_count, hop2_count, w_first, b_first, w_second, b_second,
):
    owners, cold_rows = serve_index.shape[1:]
    hot_dev, width = hot_cache.shape
    lines = hot_dev // LANES
    peers = min(PEERS, owners)
    groups = owners // peers
    teams = [[g * peers + p for p in range(peers)] for g in range(groups)]
    seeds, targets, fan = hop2_slot.shape
    half = (fan + 1) // 2
    step = (targets + 1) * seeds
    own_slot = target_slot.T
    near_slot = jnp.transpose(hop2_slot, (1, 2, 0))
    count_t = hop2_count.T

    packs = list(pl.pallas_call(
        pack_kernel,
        out_shape=[
            jax.ShapeDtypeStruct(
                ((hot_dev if g > 0 else 0) + peers * cold_rows, width), hot_cache.dtype
            )
            for g in range(groups)
        ],
        in_specs=[SMEM, SMEM, ANY, VMEM],
        out_specs=[VMEM] * groups,
        scratch_shapes=[
            pltpu.VMEM(cold_table.shape, jnp.float32),
            pltpu.VMEM(cold_table.shape, cold_table.dtype),
            pltpu.VMEM((cold_rows, width), jnp.float32),
            pltpu.SemaphoreType.DMA((8,)),
        ],
        name="pack",
    )(serve_index, serve_count, cold_table, hot_cache))
    for g in range(1, groups):
        pairs = [(i, i ^ (g * peers)) for i in range(owners)]
        packs[g] = lax.ppermute(packs[g], "gx", pairs)

    rank, ask = pl.pallas_call(
        rank_kernel,
        out_shape=(
            jax.ShapeDtypeStruct((owners * lines, LANES), jnp.float32),
            jax.ShapeDtypeStruct((peers, groups * lines, LANES), jnp.float32),
        ),
        in_specs=[VMEM, VMEM],
        out_specs=(VMEM, VMEM),
        scratch_shapes=[pltpu.VMEM((owners, lines, LANES), jnp.float32)],
        name="rank",
    )(own_slot, near_slot)
    asked = lax.all_to_all(
        ask, "gx", split_axis=0, concat_axis=0, axis_index_groups=teams, tiled=True
    )

    answer = pl.pallas_call(
        select_kernel,
        out_shape=jax.ShapeDtypeStruct(
            (peers, groups * (HOT_REQ + cold_rows), width), hot_cache.dtype
        ),
        in_specs=[VMEM] * (2 + groups),
        out_specs=VMEM,
        name="select",
    )(in_vmem(asked), hot_cache, packs[0], *map(in_vmem, packs[1:]))
    received = lax.all_to_all(
        answer, "gx", split_axis=0, concat_axis=0, axis_index_groups=teams, tiled=True
    )

    slots, place = pl.pallas_call(
        functools.partial(remap_kernel, peers, owners, cold_rows, half),
        out_shape=(
            jax.ShapeDtypeStruct(((fan + 1) * (targets + 1), seeds), jnp.int32),
            jax.ShapeDtypeStruct((targets, seeds), jnp.int32),
        ),
        in_specs=[VMEM] * 5,
        out_specs=(VMEM, VMEM),
        name="remap",
    )(own_slot, near_slot, count_t, hop1_count[None], rank)
    first, second, sizes = pl.pallas_call(
        plan_kernel,
        out_shape=(
            jax.ShapeDtypeStruct((step,), jnp.int32),
            jax.ShapeDtypeStruct((step,), jnp.int32),
            jax.ShapeDtypeStruct((2,), jnp.int32),
        ),
        in_specs=[SMEM, SMEM],
        out_specs=(SMEM, SMEM, SMEM),
        name="plan",
    )(hop1_count, place.reshape(-1))

    rows = owners * (HOT_REQ + cold_rows)
    return pl.pallas_call(
        functools.partial(finish_kernel, half),
        out_shape=jax.ShapeDtypeStruct((seeds, w_second.shape[1]), jnp.float32),
        in_specs=[ANY] + [SMEM] * 3 + [VMEM] * 3 + [ANY, VMEM, ANY, VMEM],
        out_specs=VMEM,
        scratch_shapes=[
            pltpu.VMEM((rows + 8, width), jnp.float32),
            pltpu.VMEM((step, width), jnp.float32),
            pltpu.VMEM((step, width), jnp.float32),
            pltpu.SMEM(((fan + 1) * step,), jnp.int32),
            pltpu.VMEM(w_first.shape, w_first.dtype),
            pltpu.VMEM(w_second.shape, w_second.dtype),
            pltpu.SemaphoreType.DMA((4,)),
        ],
        name="finish",
    )(
        slots.reshape(-1), first, second, sizes, in_vmem(received.reshape(rows, width)),
        hop2_count, hop1_count[:, None],
        w_first, b_first[None], w_second, b_second[None],
    )


def solution(mesh):
    return jax.shard_map(
        forward,
        mesh=mesh,
        in_specs=(
            P("gx", None), P("gx", None), P("gx", None, None), P("gx", None), P("gx", None),
            P("gx", None, None), P("gx"), P("gx", None), P(), P(), P(), P(),
        ),
        out_specs=P("gx", None),
        check_vma=False,
    )
```

time: 63.4 us -> 57.3 us (0.904)
  the two profiles are of different devices: /device:TPU:0 before, /device:TPU:19 now
where the time goes in v3:
time: 57.3 us; the launch traced here: 56.7 us
  Pallas kernels  33.5 us (58%)
  blocking collectives  8.76 us (15%)
  starting transfers between devices  8.35 us (15%)
  waiting for transfers between devices  4.6 us (8%)
  local copies, waits for them, and re-layouts  1.49 us (3%)
    pallas_call x1, Pallas kernels, forward(): pl.pallas_call(functools.partial(finish_kernel, half), out_shape=jax.Shap...  12.4 us
    all_to_all x1, blocking collectives, forward(): lax.all_to_all(ask, 'gx', split_axis=0, concat_axis=0, axis_index_groups=...  8.76 us
    pallas_call x1, Pallas kernels, forward(): pl.pallas_call(functools.partial(remap_kernel, peers, owners, cold_rows,...  5.63 us
    all_to_all x1, starting transfers between devices, forward(): lax.all_to_all(answer, 'gx', split_axis=0, concat_axis=0, axis_index_grou...  5.63 us
    pallas_call x1, Pallas kernels, forward(): pl.pallas_call(plan_kernel, out_shape=(jax.ShapeDtypeStruct((step,), jnp....  4.78 us
    ppermute x3, waiting for transfers between devices, forward(): packs[g] = lax.ppermute(packs[g], 'gx', pairs)  4.6 us
    pallas_call x1, Pallas kernels, forward(): pl.pallas_call(pack_kernel, out_shape=[jax.ShapeDtypeStruct(((hot_dev if...  4.56 us
    pallas_call x1, Pallas kernels, forward(): pl.pallas_call(rank_kernel, out_shape=(jax.ShapeDtypeStruct((owners * lin...  3.62 us
  transfers between devices with their start and end apart: 4, of which 1 were waited for; matrix products, arithmetic and copies ran while one was open for 3% of the time, Pallas kernels for 25%

profile of v3, /device:TPU:19, one launch (start us, length us, event | category | flops | bytes accessed | tf_op | source)
XLA Modules:
  0.0 56.7 jit_solution(8169829275648617795)
XLA Ops:
  0.0 4.6 %pack.1 = (bf16[256,128]{1,0:T(8,128)(2,1)}, bf16[768,128]{1,0:T(8,128)(2,1)}, bf16[768,128]{1,0:T(8,128)(2,1)}, bf16[768,128]{1,0:T(8,128)(2,1)}) custom-call(s32[1,32,32]{2,1,0:T(8,128)} %wanted.1, s32[1,32]{1,0:T(1,128)} %live.1, bf16[8192,128]{1,0:T(8,128)(2,1)} %table.1, bf16[512,128]{1,0:T(8,128)(2,1)} %hot.3), custom_call_target="tpu_custom_call" | custom-call | tf_op jit(solution)/shard_map/pack/pallas_call | solution.py:304
  4.6 0.0 copy-start
  4.6 0.0 copy-start.1
  4.6 1.4 %collective-permute-start = (bf16[768,128]{1,0:T(8,128)(2,1)}, bf16[768,128]{1,0:T(8,128)(2,1)S(1)}, u32[]{:S(2)}, u32[]{:S(2)}) collective-permute-start(bf16[768,128]{1,0:T(8,128)(2,1)} %get-tuple-element.24), channel_id=1, source_target_pairs={{0,8},{1,9},{2,10},{3,11},{4,12},{5,13},{6,14},{7,15},{8,0},{9,1},... | collective-permute-start | bytes 589832 | tf_op jit(solution)/shard_map/ppermute | solution.py:324
  6.0 0.1 collective-permute-start.1
  6.0 1.3 %collective-permute-start.2 = (bf16[768,128]{1,0:T(8,128)(2,1)}, bf16[768,128]{1,0:T(8,128)(2,1)S(1)}, u32[]{:S(2)}, u32[]{:S(2)}) collective-permute-start(bf16[768,128]{1,0:T(8,128)(2,1)} %get-tuple-element.26), channel_id=1, source_target_pairs={{0,24},{1,25},{2,26},{3,27},{4,28},{5,29},{6,30},{7,31},{8,16},{9,... | collective-permute-start | bytes 589832 | tf_op jit(solution)/shard_map/ppermute | solution.py:324
  7.3 3.6 %rank.1 = (f32[128,128]{1,0:T(8,128)}, f32[8,16,128]{2,1,0:T(8,128)}) custom-call(s32[11,128]{1,0:T(8,128)} %bitcast.14, s32[11,15,128]{2,1,0:T(8,128)} %bitcast.11), custom_call_target="tpu_custom_call" | custom-call | tf_op jit(solution)/shard_map/rank/pallas_call | solution.py:326
  10.9 8.8 %all_to_all.10.asked = f32[8,16,128]{2,1,0:T(8,128)S(1)} all-to-all(f32[8,16,128]{2,1,0:T(8,128)} %get-tuple-element.22), channel_id=1, replica_groups={{0,1,2,3,4,5,6,7},{8,9,10,11,12,13,14,15},{16,17,18,19,20,21,22,23},{24..., dimensions={0} | all-to-all | bytes 131072 | tf_op jit(solution)/shard_map/all_to_all | solution.py:337
  19.7 0.0 collective-permute-done.refs_1_
  19.7 0.0 collective-permute-done.1.refs_2_
  19.7 4.6 %collective-permute-done.2.refs_3_ = bf16[768,128]{1,0:T(8,128)(2,1)S(1)} collective-permute-done((bf16[768,128]{1,0:T(8,128)(2,1)}, bf16[768,128]{1,0:T(8,128)(2,1)S(1)}, u32[]{:S(2)}, u32[]{:S(2)}) %collective-permute-start.2) | collective-permute-done | bytes 196640 | tf_op jit(solution)/shard_map/ppermute | solution.py:324
  24.3 2.5 %select.1 = bf16[8,384,128]{2,1,0:T(8,128)(2,1)} custom-call(f32[8,16,128]{2,1,0:T(8,128)S(1)} %all_to_all.10.asked, bf16[512,128]{1,0:T(8,128)(2,1)} %hot.3, bf16[256,128]{1,0:T(8,128)(2,1)} %get-tuple-element.23.refs_0_, bf16[768,128]{1,0:T(8,128)(2,1)S(1)} %collective-permute-done.refs_1_, bf16[768,128]{1,0:T(8,128)(2,1)S(1)} %collective-permute-done.1.refs_2_, ...), custom_call_target="tpu_custom_call" | custom-call | tf_op jit(solution)/shard_map/select/pallas_call | solution.py:341
  26.8 5.6 %all-to-all-start.1 = ((bf16[8,384,128]{2,1,0:T(8,128)(2,1)}), bf16[8,384,128]{2,1,0:T(8,128)(2,1)S(1)}, u32[]{:S(2)}, u32[]{:S(2)}) async-start(bf16[8,384,128]{2,1,0:T(8,128)(2,1)} %select.1), calls=%async_computation.1 | async-start | bytes 1572864 | tf_op jit(solution)/shard_map/all_to_all | solution.py:350
  32.4 0.0 copy-done
  32.4 0.7 %copy.13.count_two = s32[128,11]{1,0:T(8,128)} copy(s32[128,11]{0,1:T(8,128)S(1)} %copy-done) | data formatting | bytes 11264 | tf_op args[7]
  33.2 5.6 %remap.1 = (s32[192,128]{1,0:T(8,128)}, s32[11,128]{1,0:T(8,128)}) custom-call(s32[11,128]{1,0:T(8,128)} %bitcast.15, s32[11,15,128]{2,1,0:T(8,128)} %bitcast.12, s32[11,128]{1,0:T(8,128)} %bitcast.16, s32[1,128]{1,0:T(1,128)} %bitcast.18, f32[128,128]{1,0:T(8,128)} %get-tuple-element.16.rank), custom_call_target="tpu_custom_call" | custom-call | tf_op jit(solution)/shard_map/remap/pallas_call | solution.py:354
  38.8 4.8 %plan.1 = (s32[1536]{0:T(1024)}, s32[1536]{0:T(1024)}, s32[2]{0:T(128)}) custom-call(s32[128]{0:T(128)} %hop1.1, s32[1408]{0:T(1024)} %bitcast.17), custom_call_target="tpu_custom_call" | custom-call | tf_op jit(solution)/shard_map/plan/pallas_call | solution.py:364
  43.6 0.0 copy-done.1
  43.6 0.7 %copy.14.count_one = s32[128,1]{1,0:T(8,128)} copy(s32[128,1]{0,1:T(1,128)S(1)} %bitcast.19) | data formatting | bytes 1024 | tf_op jit(solution)/shard_map/broadcast_in_dim | solution.py:394
  44.3 0.0 all-to-all-done.1
  44.3 12.4 %finish.1 = f32[128,256]{1,0:T(8,128)} custom-call(s32[24576]{0:T(1024)} %bitcast.13, s32[1536]{0:T(1024)} %get-tuple-element.19.first, s32[1536]{0:T(1024)} %get-tuple-element.20.second, s32[2]{0:T(128)} %get-tuple-element.21.sizes, bf16[3072,128]{1,0:T(8,128)(2,1)S(1)} %bitcast.10, s32[128,11]{1,0:T(8,128)} %copy.13.count_two, s32[128,1]{1,0:T(8,128)} %copy.14.count_one, ...), custom_call_target="tpu_custom_call" | custom-call | tf_op jit(solution)/shard_map/finish/pallas_call | solution.py:377
Async XLA Ops:
  4.6 27.8 %copy-start = (s32[128,11]{0,1:T(8,128)S(1)}, s32[128,11]{0,1:T(8,128)}, u32[]{:S(2)}) copy-start(s32[128,11]{0,1:T(8,128)} %param.19) | copy-start | bytes 16900
  4.6 39.0 %copy-start.1 = (s32[128]{0:T(128)S(1)}, s32[128]{0:T(128)}, u32[]{:S(2)}) copy-start(s32[128]{0:T(128)} %hop1.1) | copy-start | bytes 1540
  4.6 15.1 %collective-permute-start = (bf16[768,128]{1,0:T(8,128)(2,1)}, bf16[768,128]{1,0:T(8,128)(2,1)S(1)}, u32[]{:S(2)}, u32[]{:S(2)}) collective-permute-start(bf16[768,128]{1,0:T(8,128)(2,1)} %get-tuple-element.24), channel_id=1, source_target_pairs={{0,8},{1,9},{2,10},{3,11},{4,12},{5,13},{6,14},{7,15},{8,0},{9,1},... | collective-permute-start | bytes 589832 | tf_op jit(solution)/shard_map/ppermute | solution.py:324
  6.0 13.7 %collective-permute-start.1 = (bf16[768,128]{1,0:T(8,128)(2,1)}, bf16[768,128]{1,0:T(8,128)(2,1)S(1)}, u32[]{:S(2)}, u32[]{:S(2)}) collective-permute-start(bf16[768,128]{1,0:T(8,128)(2,1)} %get-tuple-element.25), channel_id=1, source_target_pairs={{0,16},{1,17},{2,18},{3,19},{4,20},{5,21},{6,22},{7,23},{8,24},{9,... | collective-permute-start | bytes 589832 | tf_op jit(solution)/shard_map/ppermute | solution.py:324
  6.0 18.3 %collective-permute-start.2 = (bf16[768,128]{1,0:T(8,128)(2,1)}, bf16[768,128]{1,0:T(8,128)(2,1)S(1)}, u32[]{:S(2)}, u32[]{:S(2)}) collective-permute-start(bf16[768,128]{1,0:T(8,128)(2,1)} %get-tuple-element.26), channel_id=1, source_target_pairs={{0,24},{1,25},{2,26},{3,27},{4,28},{5,29},{6,30},{7,31},{8,16},{9,... | collective-permute-start | bytes 589832 | tf_op jit(solution)/shard_map/ppermute | solution.py:324
  26.8 17.6 %all-to-all-start.1 = ((bf16[8,384,128]{2,1,0:T(8,128)(2,1)}), bf16[8,384,128]{2,1,0:T(8,128)(2,1)S(1)}, u32[]{:S(2)}, u32[]{:S(2)}) async-start(bf16[8,384,128]{2,1,0:T(8,128)(2,1)} %select.1), calls=%async_computation.1 | async-start | bytes 1572864 | tf_op jit(solution)/shard_map/all_to_all | solution.py:350

commit v4 on v3

--- a/solution.py
+++ b/solution.py
@@ -11,7 +11,7 @@
 LANES = 128
 HOT_REQ = 64
 PEERS = 8
-TASKS = 8
+TASKS = 16
 
 VMEM = pl.BlockSpec(memory_space=pltpu.VMEM)
 SMEM = pl.BlockSpec(memory_space=pltpu.SMEM)
@@ -33,7 +33,17 @@
     return jnp.where(iota == index, 1.0, 0.0).astype(jnp.bfloat16)
 
 
-def rank_kernel(own, near, rank, ask, held):
+def rank_kernel(own, near, wanted, live, table, rank, ask, held, wide, raw, stage, sems):
+    pieces = sems.shape[0]
+    size = table.shape[0] // pieces
+    copies = [
+        pltpu.make_async_copy(
+            table.at[pl.ds(i * size, size)], raw.at[pl.ds(i * size, size)], sems.at[i]
+        )
+        for i in range(pieces)
+    ]
+    for copy in copies:
+        copy.start()
     peers, groups = ask.shape[0], held.shape[0] // ask.shape[0]
     high = rank.shape[0]
     lines = high // held.shape[0]
@@ -65,71 +75,54 @@
     held[...] = value.reshape(held.shape)
     here = lax.axis_index("gx") // peers
     for p in range(peers):
-        ask[p] = jnp.concatenate([held[(here ^ g) * peers + p] for g in range(groups)], 0)
-
-
-def pack_kernel(wanted, live, table, hot, *refs):
-    (wide, raw, stage, sems), outs = refs[-4:], refs[:-4]
-    n_hot, cold_rows = hot.shape[0], stage.shape[0]
-    pieces = sems.shape[0]
-    size = table.shape[0] // pieces
-    copies = [
-        pltpu.make_async_copy(
-            table.at[pl.ds(i * size, size)], raw.at[pl.ds(i * size, size)], sems.at[i]
-        )
-        for i in range(pieces)
-    ]
-    for copy in copies:
-        copy.start()
-    for out in outs[1:]:
-        out[pl.ds(0, n_hot), :] = hot[...]
+        ask[p, 0 : groups * lines, :] = jnp.concatenate(
+            [held[(here ^ g) * peers + p] for g in range(groups)], 0
+        ).astype(ask.dtype)
+
     for i, copy in enumerate(copies):
         copy.wait()
-        here = pl.ds(i * size, size)
-        wide[here, :] = raw[here, :].astype(jnp.float32)
-    peers = outs[0].shape[0] // cold_rows
-    group = lax.axis_index("gx") // peers
+        part = pl.ds(i * size, size)
+        wide[part, :] = raw[part, :].astype(jnp.float32)
+    cold_rows = stage.shape[0]
     line = lax.broadcasted_iota(jnp.int32, stage.shape, 0)
-    for g, out in enumerate(outs):
-        base = out.shape[0] - peers * cold_rows
-
-        def one_device(p, carry, g=g, out=out, base=base):
-            d = (group ^ g) * peers + p
+    for g in range(groups):
+        place = pl.ds(groups * lines + g * cold_rows, cold_rows)
+
+        def one_device(p, carry, g=g, place=place):
+            d = (here ^ g) * peers + p
             for j in range(cold_rows):
                 stage[j : j + 1, :] = wide[pl.ds(wanted[0, d, j], 1), :]
-            kept = jnp.where(line < live[0, d], stage[...], 0.0).astype(out.dtype)
-            out[pl.ds(pl.multiple_of(base + p * cold_rows, cold_rows), cold_rows), :] = kept
+            ask[p, place, :] = jnp.where(line < live[0, d], stage[...], 0.0).astype(ask.dtype)
             return carry
 
         lax.fori_loop(0, peers, one_device, 0)
 
 
-def select_kernel(asked, hot, *refs):
-    packs, out = refs[:-1], refs[-1]
+def select_kernel(asked, *refs):
+    groups = (len(refs) - 1) // 2
+    shards, out, colds = refs[:groups], refs[groups], refs[groups + 1 :]
     peers = asked.shape[0]
-    n_hot, groups = hot.shape[0], len(packs)
-    lines = n_hot // LANES
-    cold_rows = packs[0].shape[0] // peers
+    lines = shards[0].shape[0] // LANES
+    cold_rows = colds[0].shape[0] // peers
     want = lax.broadcasted_iota(jnp.int32, (HOT_REQ, LANES), 0).astype(jnp.float32)
-    for g, pack in enumerate(packs):
-        shard = hot[...] if g == 0 else pack[0:n_hot, :]
-        first = pack.shape[0] - peers * cold_rows
+    ranks = [asked[p, 0 : groups * lines, :].astype(jnp.float32) for p in range(peers)]
+    for g, shard in enumerate(shards):
         picks = []
         for p in range(peers):
-            rows = [asked[p, g * lines + r : g * lines + r + 1, :] for r in range(lines)]
+            rows = [ranks[p][g * lines + r : g * lines + r + 1, :] for r in range(lines)]
             picks.append(
                 jnp.concatenate([jnp.where(want == row, 1.0, 0.0) for row in rows], 1).astype(
                     jnp.bfloat16
                 )
             )
         picked = jnp.dot(
-            jnp.concatenate(picks, 0), shard, preferred_element_type=jnp.float32
+            jnp.concatenate(picks, 0), shard[...], preferred_element_type=jnp.float32
         ).astype(out.dtype)
+        place = groups * lines + g * cold_rows
         for p in range(peers):
             out[p, g * HOT_REQ : (g + 1) * HOT_REQ, :] = picked[p * HOT_REQ : (p + 1) * HOT_REQ]
-            place = groups * HOT_REQ + g * cold_rows
-            out[p, place : place + cold_rows, :] = pack[
-                first + p * cold_rows : first + (p + 1) * cold_rows, :
+            colds[g][p * cold_rows : (p + 1) * cold_rows, :] = asked[
+                p, place : place + cold_rows, :
             ]
 
 
@@ -160,12 +153,14 @@
             is_cold = as_cold >= 0
             owner = jnp.where(is_cold, as_cold >> cold_bits, r >> owner_bits)
             group = (owner >> peer_bits) ^ here
-            inside = jnp.where(
+            member = owner & (peers - 1)
+            row = jnp.where(
                 is_cold,
-                groups * HOT_REQ + group * cold_rows + (as_cold & (cold_rows - 1)),
-                group * HOT_REQ + rank_here,
+                owners * HOT_REQ
+                + (group * peers + member) * cold_rows
+                + (as_cold & (cold_rows - 1)),
+                (member * groups + group) * HOT_REQ + rank_here,
             )
-            row = (owner & (peers - 1)) * (groups * per) + inside
             if k > 0:
                 row = jnp.where(count[t : t + 1, :] > k - 1, row, empty)
             out[k * stride + t : k * stride + t + 1, :] = row
@@ -217,11 +212,12 @@
 
 
 def finish_kernel(
-    half, slots_in, first, second, sizes, rows, count_two, count_one,
-    w_first_in, b_first, w_second_in, b_second, out,
-    table, own, total, slots, w_first, w_second, sems,
+    half, slots_in, first, second, sizes, count_two, count_one,
+    w_first_in, b_first, w_second_in, b_second, *refs,
 ):
-    n_rows, width = rows.shape
+    blocks = refs[:-8]
+    out, table, own, total, slots, w_first, w_second, sems = refs[-8:]
+    width = own.shape[1]
     seeds, targets = count_two.shape
     step = own.shape[0]
     per = slots.shape[0] // step
@@ -233,7 +229,10 @@
     copies.append(pltpu.make_async_copy(w_second_in, w_second, sems.at[3]))
     for copy in copies:
         copy.start()
-    table[pl.ds(0, n_rows), :] = rows[...].astype(jnp.float32)
+    n_rows = 0
+    for block in blocks:
+        table[pl.ds(n_rows, block.shape[0]), :] = block[...].astype(jnp.float32)
+        n_rows += block.shape[0]
     table[pl.ds(n_rows, 8), :] = jnp.zeros((8, width), jnp.float32)
     copies[0].wait()
 
@@ -301,55 +300,43 @@
     near_slot = jnp.transpose(hop2_slot, (1, 2, 0))
     count_t = hop2_count.T
 
-    packs = list(pl.pallas_call(
-        pack_kernel,
-        out_shape=[
-            jax.ShapeDtypeStruct(
-                ((hot_dev if g > 0 else 0) + peers * cold_rows, width), hot_cache.dtype
-            )
-            for g in range(groups)
-        ],
-        in_specs=[SMEM, SMEM, ANY, VMEM],
-        out_specs=[VMEM] * groups,
+    swaps = [[(i, i ^ (g * peers)) for i in range(owners)] for g in range(groups)]
+    shards = [hot_cache]
+    for g in range(1, groups):
+        shards.append(lax.ppermute(hot_cache, "gx", swaps[g]))
+    rank, ask = pl.pallas_call(
+        rank_kernel,
+        out_shape=(
+            jax.ShapeDtypeStruct((owners * lines, LANES), jnp.float32),
+            jax.ShapeDtypeStruct((peers, groups * (lines + cold_rows), width), jnp.bfloat16),
+        ),
+        in_specs=[VMEM, VMEM, SMEM, SMEM, ANY],
+        out_specs=(VMEM, VMEM),
         scratch_shapes=[
+            pltpu.VMEM((owners, lines, LANES), jnp.float32),
             pltpu.VMEM(cold_table.shape, jnp.float32),
             pltpu.VMEM(cold_table.shape, cold_table.dtype),
             pltpu.VMEM((cold_rows, width), jnp.float32),
             pltpu.SemaphoreType.DMA((8,)),
         ],
-        name="pack",
-    )(serve_index, serve_count, cold_table, hot_cache))
-    for g in range(1, groups):
-        pairs = [(i, i ^ (g * peers)) for i in range(owners)]
-        packs[g] = lax.ppermute(packs[g], "gx", pairs)
-
-    rank, ask = pl.pallas_call(
-        rank_kernel,
-        out_shape=(
-            jax.ShapeDtypeStruct((owners * lines, LANES), jnp.float32),
-            jax.ShapeDtypeStruct((peers, groups * lines, LANES), jnp.float32),
-        ),
-        in_specs=[VMEM, VMEM],
-        out_specs=(VMEM, VMEM),
-        scratch_shapes=[pltpu.VMEM((owners, lines, LANES), jnp.float32)],
         name="rank",
-    )(own_slot, near_slot)
+    )(own_slot, near_slot, serve_index, serve_count, cold_table)
     asked = lax.all_to_all(
         ask, "gx", split_axis=0, concat_axis=0, axis_index_groups=teams, tiled=True
     )
-
-    answer = pl.pallas_call(
+    answer, *colds = pl.pallas_call(
         select_kernel,
-        out_shape=jax.ShapeDtypeStruct(
-            (peers, groups * (HOT_REQ + cold_rows), width), hot_cache.dtype
-        ),
-        in_specs=[VMEM] * (2 + groups),
-        out_specs=VMEM,
+        out_shape=[jax.ShapeDtypeStruct((peers, groups * HOT_REQ, width), hot_cache.dtype)]
+        + [jax.ShapeDtypeStruct((peers * cold_rows, width), hot_cache.dtype)] * groups,
+        in_specs=[VMEM] * (1 + groups),
+        out_specs=[VMEM] * (1 + groups),
         name="select",
-    )(in_vmem(asked), hot_cache, packs[0], *map(in_vmem, packs[1:]))
+    )(in_vmem(asked), hot_cache, *map(in_vmem, shards[1:]))
     received = lax.all_to_all(
         answer, "gx", split_axis=0, concat_axis=0, axis_index_groups=teams, tiled=True
     )
+    for g in range(1, groups):
+        colds[g] = lax.ppermute(colds[g], "gx", swaps[g])
 
     slots, place = pl.pallas_call(
         functools.partial(remap_kernel, peers, owners, cold_rows, half),
@@ -377,7 +364,7 @@
     return pl.pallas_call(
         functools.partial(finish_kernel, half),
         out_shape=jax.ShapeDtypeStruct((seeds, w_second.shape[1]), jnp.float32),
-        in_specs=[ANY] + [SMEM] * 3 + [VMEM] * 3 + [ANY, VMEM, ANY, VMEM],
+        in_specs=[ANY] + [SMEM] * 3 + [VMEM] * 2 + [ANY, VMEM, ANY, VMEM] + [VMEM] * (1 + groups),
         out_specs=VMEM,
         scratch_shapes=[
             pltpu.VMEM((rows + 8, width), jnp.float32),
@@ -390,9 +377,9 @@
         ],
         name="finish",
     )(
-        slots.reshape(-1), first, second, sizes, in_vmem(received.reshape(rows, width)),
-        hop2_count, hop1_count[:, None],
+        in_vmem(slots.reshape(-1)), first, second, sizes, hop2_count, hop1_count[:, None],
         w_first, b_first[None], w_second, b_second[None],
+        in_vmem(received.reshape(owners * HOT_REQ, width)), colds[0], *map(in_vmem, colds[1:]),
     )
 
 

time: 57.3 us -> 61.8 us (1.079)
  the two profiles are of different devices: /device:TPU:19 before, /device:TPU:0 now
where the time goes in v4:
time: 61.8 us; the launch traced here: 61.3 us
  Pallas kernels  30.2 us (49%)
  starting transfers between devices  18.5 us (30%)
  waiting for transfers between devices  10.1 us (16%)
  local copies, waits for them, and re-layouts  2.36 us (4%)
    pallas_call x1, Pallas kernels, forward(): pl.pallas_call(functools.partial(finish_kernel, half), out_shape=jax.Shap...  11.9 us
    ppermute x3, waiting for transfers between devices, forward(): shards.append(lax.ppermute(hot_cache, 'gx', swaps[g]))  10.1 us
    pallas_call x1, Pallas kernels, forward(): pl.pallas_call(functools.partial(remap_kernel, peers, owners, cold_rows,...  5.7 us
    pallas_call x1, Pallas kernels, forward(): pl.pallas_call(rank_kernel, out_shape=(jax.ShapeDtypeStruct((owners * lin...  5.44 us
    all_to_all x1, starting transfers between devices, forward(): lax.all_to_all(ask, 'gx', split_axis=0, concat_axis=0, axis_index_groups=...  5.22 us
    pallas_call x1, Pallas kernels, forward(): pl.pallas_call(plan_kernel, out_shape=(jax.ShapeDtypeStruct((step,), jnp....  4.79 us
    ppermute x3, starting transfers between devices, forward(): colds[g] = lax.ppermute(colds[g], 'gx', swaps[g])  4.76 us
    ppermute x3, starting transfers between devices, forward(): shards.append(lax.ppermute(hot_cache, 'gx', swaps[g]))  4.45 us
  transfers between devices with their start and end apart: 8, of which 2 were waited for; matrix products, arithmetic and copies ran while one was open for 2% of the time, Pallas kernels for 17%

profile of v4, /device:TPU:0, one launch (start us, length us, event | category | flops | bytes accessed | tf_op | source)
XLA Modules:
  0.0 61.3 jit_solution(7489788516110644329)
XLA Ops:
  0.0 0.0 copy-start.1
  0.0 0.0 copy-start.2
  0.0 0.0 copy-start.3
  0.0 5.4 %rank.1 = (f32[128,128]{1,0:T(8,128)}, bf16[8,144,128]{2,1,0:T(8,128)(2,1)}) custom-call(s32[11,128]{1,0:T(8,128)} %bitcast.14, s32[11,15,128]{2,1,0:T(8,128)} %bitcast.12, s32[1,32,32]{2,1,0:T(8,128)} %wanted.1, s32[1,32]{1,0:T(1,128)} %live.1, bf16[8192,128]{1,0:T(8,128)(2,1)} %table.1), custom_call_target="tpu_custom_call" | custom-call | tf_op jit(solution)/shard_map/rank/pallas_call | solution.py:307
  5.5 5.2 %all-to-all-start = ((bf16[8,144,128]{2,1,0:T(8,128)(2,1)}), bf16[8,144,128]{2,1,0:T(8,128)(2,1)S(1)}, u32[]{:S(2)}, u32[]{:S(2)}) async-start(bf16[8,144,128]{2,1,0:T(8,128)(2,1)} %get-tuple-element.23), calls=%async_computation | async-start | bytes 589824 | tf_op jit(solution)/shard_map/all_to_all | solution.py:324
  10.7 0.0 copy-done.1
  10.7 1.6 %collective-permute-start = (bf16[512,128]{1,0:T(8,128)(2,1)S(1)}, bf16[512,128]{1,0:T(8,128)(2,1)S(1)}, u32[]{:S(2)}, u32[]{:S(2)}) collective-permute-start(bf16[512,128]{1,0:T(8,128)(2,1)S(1)} %copy-done.1), channel_id=1, source_target_pairs={{0,8},{1,9},{2,10},{3,11},{4,12},{5,13},{6,14},{7,15},{8,0},{9,1},... | collective-permute-start | bytes 393224 | tf_op jit(solution)/shard_map/ppermute | solution.py:306
  12.3 2.6 %collective-permute-start.1 = (bf16[512,128]{1,0:T(8,128)(2,1)S(1)}, bf16[512,128]{1,0:T(8,128)(2,1)S(1)}, u32[]{:S(2)}, u32[]{:S(2)}) collective-permute-start(bf16[512,128]{1,0:T(8,128)(2,1)S(1)} %copy-done.1), channel_id=1, source_target_pairs={{0,16},{1,17},{2,18},{3,19},{4,20},{5,21},{6,22},{7,23},{8,24},{9,... | collective-permute-start | bytes 393224 | tf_op jit(solution)/shard_map/ppermute | solution.py:306
  14.9 0.2 collective-permute-start.2
  15.1 3.7 %collective-permute-done.refs_1_ = bf16[512,128]{1,0:T(8,128)(2,1)S(1)} collective-permute-done((bf16[512,128]{1,0:T(8,128)(2,1)S(1)}, bf16[512,128]{1,0:T(8,128)(2,1)S(1)}, u32[]{:S(2)}, u32[]{:S(2)}) %collective-permute-start) | collective-permute-done | bytes 131104 | tf_op jit(solution)/shard_map/ppermute | solution.py:306
  18.8 6.5 %collective-permute-done.1.refs_2_ = bf16[512,128]{1,0:T(8,128)(2,1)S(1)} collective-permute-done((bf16[512,128]{1,0:T(8,128)(2,1)S(1)}, bf16[512,128]{1,0:T(8,128)(2,1)S(1)}, u32[]{:S(2)}, u32[]{:S(2)}) %collective-permute-start.1) | collective-permute-done | bytes 131104 | tf_op jit(solution)/shard_map/ppermute | solution.py:306
  25.3 0.0 collective-permute-done.2.refs_3_
  25.3 0.0 all-to-all-done.asked
  25.3 2.4 %select.1 = (bf16[8,256,128]{2,1,0:T(8,128)(2,1)}, bf16[256,128]{1,0:T(8,128)(2,1)}, bf16[256,128]{1,0:T(8,128)(2,1)}, bf16[256,128]{1,0:T(8,128)(2,1)}, bf16[256,128]{1,0:T(8,128)(2,1)}) custom-call(bf16[8,144,128]{2,1,0:T(8,128)(2,1)S(1)} %all-to-all-done.asked, bf16[512,128]{1,0:T(8,128)(2,1)} %refs_0_.1, ...), custom_call_target="tpu_custom_call" | custom-call | tf_op jit(solution)/shard_map/select/pallas_call | solution.py:327
  27.7 4.1 %all-to-all-start.1 = ((bf16[8,256,128]{2,1,0:T(8,128)(2,1)}), bf16[8,256,128]{2,1,0:T(8,128)(2,1)S(1)}, u32[]{:S(2)}, u32[]{:S(2)}) async-start(bf16[8,256,128]{2,1,0:T(8,128)(2,1)} %get-tuple-element.24), calls=%async_computation.1 | async-start | bytes 1048576 | tf_op jit(solution)/shard_map/all_to_all | solution.py:335
  31.8 2.3 %collective-permute-start.3 = (bf16[256,128]{1,0:T(8,128)(2,1)}, bf16[256,128]{1,0:T(8,128)(2,1)S(1)}, u32[]{:S(2)}, u32[]{:S(2)}) collective-permute-start(bf16[256,128]{1,0:T(8,128)(2,1)} %get-tuple-element.26), channel_id=1, source_target_pairs={{0,8},{1,9},{2,10},{3,11},{4,12},{5,13},{6,14},{7,15},{8,0},{9,1},... | collective-permute-start | bytes 196616 | tf_op jit(solution)/shard_map/ppermute | solution.py:339
  34.0 1.1 %collective-permute-start.4 = (bf16[256,128]{1,0:T(8,128)(2,1)}, bf16[256,128]{1,0:T(8,128)(2,1)S(1)}, u32[]{:S(2)}, u32[]{:S(2)}) collective-permute-start(bf16[256,128]{1,0:T(8,128)(2,1)} %get-tuple-element.27), channel_id=1, source_target_pairs={{0,16},{1,17},{2,18},{3,19},{4,20},{5,21},{6,22},{7,23},{8,24},{9,... | collective-permute-start | bytes 196616 | tf_op jit(solution)/shard_map/ppermute | solution.py:339
  35.1 1.4 %collective-permute-start.5 = (bf16[256,128]{1,0:T(8,128)(2,1)}, bf16[256,128]{1,0:T(8,128)(2,1)S(1)}, u32[]{:S(2)}, u32[]{:S(2)}) collective-permute-start(bf16[256,128]{1,0:T(8,128)(2,1)} %get-tuple-element.28), channel_id=1, source_target_pairs={{0,24},{1,25},{2,26},{3,27},{4,28},{5,29},{6,30},{7,31},{8,16},{9,... | collective-permute-start | bytes 196616 | tf_op jit(solution)/shard_map/ppermute | solution.py:339
  36.5 0.0 copy-done.2
  36.5 0.7 %copy.13.count_two = s32[128,11]{1,0:T(8,128)} copy(s32[128,11]{0,1:T(8,128)S(1)} %copy-done.2) | data formatting | bytes 11264 | tf_op args[7]
  37.3 5.7 %remap.1 = (s32[192,128]{1,0:T(8,128)}, s32[11,128]{1,0:T(8,128)}) custom-call(s32[11,128]{1,0:T(8,128)} %bitcast.15, s32[11,15,128]{2,1,0:T(8,128)} %bitcast.13, s32[11,128]{1,0:T(8,128)} %bitcast.16, s32[1,128]{1,0:T(1,128)} %bitcast.18, f32[128,128]{1,0:T(8,128)} %get-tuple-element.17.rank), custom_call_target="tpu_custom_call" | custom-call | tf_op jit(solution)/shard_map/remap/pallas_call | solution.py:341
  42.9 4.8 %plan.1 = (s32[1536]{0:T(1024)}, s32[1536]{0:T(1024)}, s32[2]{0:T(128)}) custom-call(s32[128]{0:T(128)} %hop1.1, s32[1408]{0:T(1024)} %bitcast.17), custom_call_target="tpu_custom_call" | custom-call | tf_op jit(solution)/shard_map/plan/pallas_call | solution.py:351
  47.7 0.0 copy-done.3
  47.8 0.7 %copy.14.count_one = s32[128,1]{1,0:T(8,128)} copy(s32[128,1]{0,1:T(1,128)S(1)} %bitcast.19) | data formatting | bytes 1024 | tf_op jit(solution)/shard_map/broadcast_in_dim | solution.py:380
  48.5 0.0 collective-permute-done.3.refs_2_
  48.5 0.0 collective-permute-done.4.refs_3_
  48.5 0.0 collective-permute-done.5.refs_4_
  48.5 0.0 all-to-all-done.1
  48.5 0.0 copy-start
  48.5 0.9 %copy-done = s32[192,128]{1,0:T(8,128)S(1)} copy-done((s32[192,128]{1,0:T(8,128)S(1)}, s32[192,128]{1,0:T(8,128)}, u32[]{:S(2)}) %copy-start) | copy-done | bytes 98328
  49.4 11.9 %finish.1 = f32[128,256]{1,0:T(8,128)} custom-call(s32[24576]{0:T(1024)S(1)} %bitcast.11, s32[1536]{0:T(1024)} %get-tuple-element.20.first, s32[1536]{0:T(1024)} %get-tuple-element.21.second, s32[2]{0:T(128)} %get-tuple-element.22.sizes, s32[128,11]{1,0:T(8,128)} %copy.13.count_two, s32[128,1]{1,0:T(8,128)} %copy.14.count_one, bf16[256,256]{1,0:T(8,128)(2,1)} %w_first_in.1, ...), custom_call_target="tpu_custom_call" | custom-call | tf_op jit(solution)/shard_map/finish/pallas_call | solution.py:364
Async XLA Ops:
  0.0 10.7 %copy-start.1 = (bf16[512,128]{1,0:T(8,128)(2,1)S(1)}, bf16[512,128]{1,0:T(8,128)(2,1)}, u32[]{:S(2)}) copy-start(bf16[512,128]{1,0:T(8,128)(2,1)} %refs_0_.1) | copy-start | bytes 393220
  0.0 36.5 %copy-start.2 = (s32[128,11]{0,1:T(8,128)S(1)}, s32[128,11]{0,1:T(8,128)}, u32[]{:S(2)}) copy-start(s32[128,11]{0,1:T(8,128)} %param.19) | copy-start | bytes 16900
  0.0 47.7 %copy-start.3 = (s32[128]{0:T(128)S(1)}, s32[128]{0:T(128)}, u32[]{:S(2)}) copy-start(s32[128]{0:T(128)} %hop1.1) | copy-start | bytes 1540
  5.5 19.8 %all-to-all-start = ((bf16[8,144,128]{2,1,0:T(8,128)(2,1)}), bf16[8,144,128]{2,1,0:T(8,128)(2,1)S(1)}, u32[]{:S(2)}, u32[]{:S(2)}) async-start(bf16[8,144,128]{2,1,0:T(8,128)(2,1)} %get-tuple-element.23), calls=%async_computation | async-start | bytes 589824 | tf_op jit(solution)/shard_map/all_to_all | solution.py:324
  10.7 8.1 %collective-permute-start = (bf16[512,128]{1,0:T(8,128)(2,1)S(1)}, bf16[512,128]{1,0:T(8,128)(2,1)S(1)}, u32[]{:S(2)}, u32[]{:S(2)}) collective-permute-start(bf16[512,128]{1,0:T(8,128)(2,1)S(1)} %copy-done.1), channel_id=1, source_target_pairs={{0,8},{1,9},{2,10},{3,11},{4,12},{5,13},{6,14},{7,15},{8,0},{9,1},... | collective-permute-start | bytes 393224 | tf_op jit(solution)/shard_map/ppermute | solution.py:306
  12.3 12.9 %collective-permute-start.1 = (bf16[512,128]{1,0:T(8,128)(2,1)S(1)}, bf16[512,128]{1,0:T(8,128)(2,1)S(1)}, u32[]{:S(2)}, u32[]{:S(2)}) collective-permute-start(bf16[512,128]{1,0:T(8,128)(2,1)S(1)} %copy-done.1), channel_id=1, source_target_pairs={{0,16},{1,17},{2,18},{3,19},{4,20},{5,21},{6,22},{7,23},{8,24},{9,... | collective-permute-start | bytes 393224 | tf_op jit(solution)/shard_map/ppermute | solution.py:306
  14.9 10.3 %collective-permute-start.2 = (bf16[512,128]{1,0:T(8,128)(2,1)S(1)}, bf16[512,128]{1,0:T(8,128)(2,1)S(1)}, u32[]{:S(2)}, u32[]{:S(2)}) collective-permute-start(bf16[512,128]{1,0:T(8,128)(2,1)S(1)} %copy-done.1), channel_id=1, source_target_pairs={{0,24},{1,25},{2,26},{3,27},{4,28},{5,29},{6,30},{7,31},{8,16},{9,... | collective-permute-start | bytes 393224 | tf_op jit(solution)/shard_map/ppermute | solution.py:306
  27.7 20.8 %all-to-all-start.1 = ((bf16[8,256,128]{2,1,0:T(8,128)(2,1)}), bf16[8,256,128]{2,1,0:T(8,128)(2,1)S(1)}, u32[]{:S(2)}, u32[]{:S(2)}) async-start(bf16[8,256,128]{2,1,0:T(8,128)(2,1)} %get-tuple-element.24), calls=%async_computation.1 | async-start | bytes 1048576 | tf_op jit(solution)/shard_map/all_to_all | solution.py:335
  31.8 16.7 %collective-permute-start.3 = (bf16[256,128]{1,0:T(8,128)(2,1)}, bf16[256,128]{1,0:T(8,128)(2,1)S(1)}, u32[]{:S(2)}, u32[]{:S(2)}) collective-permute-start(bf16[256,128]{1,0:T(8,128)(2,1)} %get-tuple-element.26), channel_id=1, source_target_pairs={{0,8},{1,9},{2,10},{3,11},{4,12},{5,13},{6,14},{7,15},{8,0},{9,1},... | collective-permute-start | bytes 196616 | tf_op jit(solution)/shard_map/ppermute | solution.py:339
  34.0 14.5 %collective-permute-start.4 = (bf16[256,128]{1,0:T(8,128)(2,1)}, bf16[256,128]{1,0:T(8,128)(2,1)S(1)}, u32[]{:S(2)}, u32[]{:S(2)}) collective-permute-start(bf16[256,128]{1,0:T(8,128)(2,1)} %get-tuple-element.27), channel_id=1, source_target_pairs={{0,16},{1,17},{2,18},{3,19},{4,20},{5,21},{6,22},{7,23},{8,24},{9,... | collective-permute-start | bytes 196616 | tf_op jit(solution)/shard_map/ppermute | solution.py:339
  35.1 13.4 %collective-permute-start.5 = (bf16[256,128]{1,0:T(8,128)(2,1)}, bf16[256,128]{1,0:T(8,128)(2,1)S(1)}, u32[]{:S(2)}, u32[]{:S(2)}) collective-permute-start(bf16[256,128]{1,0:T(8,128)(2,1)} %get-tuple-element.28), channel_id=1, source_target_pairs={{0,24},{1,25},{2,26},{3,27},{4,28},{5,29},{6,30},{7,31},{8,16},{9,... | collective-permute-start | bytes 196616 | tf_op jit(solution)/shard_map/ppermute | solution.py:339
  48.5 0.9 %copy-start = (s32[192,128]{1,0:T(8,128)S(1)}, s32[192,128]{1,0:T(8,128)}, u32[]{:S(2)}) copy-start(s32[192,128]{1,0:T(8,128)} %get-tuple-element.18) | copy-start | bytes 294916

commit v5 on v4

--- a/solution.py
+++ b/solution.py
@@ -11,7 +11,7 @@
 LANES = 128
 HOT_REQ = 64
 PEERS = 8
-TASKS = 16
+TASKS = 32
 
 VMEM = pl.BlockSpec(memory_space=pltpu.VMEM)
 SMEM = pl.BlockSpec(memory_space=pltpu.SMEM)
@@ -29,8 +29,11 @@
 
 
 def one_hot(index, size):
-    iota = lax.broadcasted_iota(jnp.int32, (size, index.shape[1]), 0)
-    return jnp.where(iota == index, 1.0, 0.0).astype(jnp.bfloat16)
+    iota = lax.broadcasted_iota(jnp.int16, (size, index.shape[1]), 0)
+    wide = jnp.broadcast_to(index, iota.shape[:0] + (16, index.shape[1])).astype(jnp.int16)
+    wide = jnp.concatenate([wide] * (size // 16), 0)
+    one, zero = jnp.ones((), jnp.bfloat16), jnp.zeros((), jnp.bfloat16)
+    return jnp.where(iota == wide, one, zero)
 
 
 def rank_kernel(own, near, wanted, live, table, rank, ask, held, wide, raw, stage, sems):
@@ -126,7 +129,7 @@
             ]
 
 
-def remap_kernel(peers, owners, cold_rows, half, own, near, count, ones, rank, out, place):
+def remap_kernel(peers, owners, cold_rows, half, own, near, count, ones, rank, out, place, sizes):
     high = rank.shape[0]
     targets, fan = near.shape[0], near.shape[1]
     stride = out.shape[0] // (fan + 1)
@@ -179,6 +182,10 @@
         spots.append(spot[t : t + 1, :] + upper)
         upper = upper + more[t : t + 1, :]
     place[...] = jnp.concatenate(spots, 0).astype(jnp.int32)
+    both = jnp.concatenate(
+        [count[...], ones[...], jnp.zeros((LANES - targets - 1, LANES), jnp.int32)], 0
+    )
+    sizes[...] = jnp.transpose(both.astype(jnp.float32))
 
 
 def plan_kernel(hop1, place, first, second, sizes):
@@ -212,13 +219,13 @@
 
 
 def finish_kernel(
-    half, slots_in, first, second, sizes, count_two, count_one,
+    half, targets, slots_in, first, second, sizes, counts,
     w_first_in, b_first, w_second_in, b_second, *refs,
 ):
-    blocks = refs[:-8]
-    out, table, own, total, slots, w_first, w_second, sems = refs[-8:]
+    blocks = refs[:-9]
+    out, table, own, total, extra, slots, w_first, w_second, sems = refs[-9:]
     width = own.shape[1]
-    seeds, targets = count_two.shape
+    seeds = counts.shape[0]
     step = own.shape[0]
     per = slots.shape[0] // step
     copies = [
@@ -234,6 +241,7 @@
         table[pl.ds(n_rows, block.shape[0]), :] = block[...].astype(jnp.float32)
         n_rows += block.shape[0]
     table[pl.ds(n_rows, 8), :] = jnp.zeros((8, width), jnp.float32)
+    extra[...] = jnp.zeros(extra.shape, jnp.float32)
     copies[0].wait()
 
     parts = [slots.at[pl.ds(k * step, step)] for k in range(per)]
@@ -249,13 +257,9 @@
         return carry
 
     def second_part(i, carry):
-        codes = [second[i * TASKS + g] for g in range(TASKS)]
-        held = [total[pl.ds(code, 1), :] for code in codes]
-        sums = [
-            h + tree([pick(k, code) for k in range(half, per)]) for h, code in zip(held, codes)
-        ]
-        for code, value in zip(codes, sums):
-            total[pl.ds(code, 1), :] = value
+        for g in range(TASKS):
+            code = second[i * TASKS + g]
+            extra[pl.ds(code, 1), :] = tree([pick(k, code) for k in range(half, per)])
         return carry
 
     lax.fori_loop(0, sizes[0], first_part, 0)
@@ -265,10 +269,10 @@
     copies[3].wait()
 
     pooled = jnp.zeros((seeds, w_first.shape[1]), jnp.float32)
-    near = count_one[...]
+    near = counts[:, targets : targets + 1]
     for t in range(targets):
         here = pl.ds(t * seeds, seeds)
-        aggregate = total[here, :] / count_two[:, t : t + 1].astype(jnp.float32)
+        aggregate = (total[here, :] + extra[here, :]) / counts[:, t : t + 1]
         stacked = jnp.concatenate(
             [own[here, :].astype(jnp.bfloat16), aggregate.astype(jnp.bfloat16)], -1
         )
@@ -278,7 +282,7 @@
             seed_hidden = hidden
         else:
             pooled += jnp.where(near > t - 1, hidden.astype(jnp.float32), 0.0)
-    pooled = (pooled / near.astype(jnp.float32)).astype(jnp.bfloat16)
+    pooled = (pooled / near).astype(jnp.bfloat16)
     joined = jnp.concatenate([seed_hidden, pooled], -1)
     out[...] = jnp.dot(joined, w_second[...], preferred_element_type=jnp.float32) + b_second[...]
 
@@ -331,21 +335,22 @@
         in_specs=[VMEM] * (1 + groups),
         out_specs=[VMEM] * (1 + groups),
         name="select",
-    )(in_vmem(asked), hot_cache, *map(in_vmem, shards[1:]))
+    )(in_vmem(asked), in_vmem(hot_cache), *map(in_vmem, shards[1:]))
     received = lax.all_to_all(
         answer, "gx", split_axis=0, concat_axis=0, axis_index_groups=teams, tiled=True
     )
     for g in range(1, groups):
         colds[g] = lax.ppermute(colds[g], "gx", swaps[g])
 
-    slots, place = pl.pallas_call(
+    slots, place, counts = pl.pallas_call(
         functools.partial(remap_kernel, peers, owners, cold_rows, half),
         out_shape=(
             jax.ShapeDtypeStruct(((fan + 1) * (targets + 1), seeds), jnp.int32),
             jax.ShapeDtypeStruct((targets, seeds), jnp.int32),
+            jax.ShapeDtypeStruct((seeds, LANES), jnp.float32),
         ),
         in_specs=[VMEM] * 5,
-        out_specs=(VMEM, VMEM),
+        out_specs=(VMEM, VMEM, VMEM),
         name="remap",
     )(own_slot, near_slot, count_t, hop1_count[None], rank)
     first, second, sizes = pl.pallas_call(
@@ -362,12 +367,13 @@
 
     rows = owners * (HOT_REQ + cold_rows)
     return pl.pallas_call(
-        functools.partial(finish_kernel, half),
+        functools.partial(finish_kernel, half, targets),
         out_shape=jax.ShapeDtypeStruct((seeds, w_second.shape[1]), jnp.float32),
-        in_specs=[ANY] + [SMEM] * 3 + [VMEM] * 2 + [ANY, VMEM, ANY, VMEM] + [VMEM] * (1 + groups),
+        in_specs=[ANY] + [SMEM] * 3 + [VMEM] + [ANY, VMEM, ANY, VMEM] + [VMEM] * (1 + groups),
         out_specs=VMEM,
         scratch_shapes=[
             pltpu.VMEM((rows + 8, width), jnp.float32),
+            pltpu.VMEM((step, width), jnp.float32),
             pltpu.VMEM((step, width), jnp.float32),
             pltpu.VMEM((step, width), jnp.float32),
             pltpu.SMEM(((fan + 1) * step,), jnp.int32),
@@ -377,7 +383,7 @@
         ],
         name="finish",
     )(
-        in_vmem(slots.reshape(-1)), first, second, sizes, hop2_count, hop1_count[:, None],
+        slots.reshape(-1), first, second, sizes, counts,
         w_first, b_first[None], w_second, b_second[None],
         in_vmem(received.reshape(owners * HOT_REQ, width)), colds[0], *map(in_vmem, colds[1:]),
     )

time: 61.8 us -> 57.3 us (0.927)
  local copies, waits for them, and re-layouts: 2.36 us -> 0.01 us
  Pallas kernels: 30.2 us -> 28.4 us
  waiting for transfers between devices: 10.1 us -> 9.14 us
  starting transfers between devices: 18.5 us -> 19.2 us
    unnamed x9 -> x2, local copies, waits for them, and re-layouts: 1.62 us -> 0.01 us
    ppermute x3, waiting for transfers between devices: 10.1 us -> 9.12 us  [forward(): shards.append(lax.ppermute(hot_cache, 'gx', swaps[g]))]
    ppermute x3, starting transfers between devices: 4.76 us -> 5.71 us  [forward(): colds[g] = lax.ppermute(colds[g], 'gx', swaps[g])]
    pallas_call x1, Pallas kernels: 2.41 us -> 1.5 us  [forward(): pl.pallas_call(select_kernel, out_shape=[jax.ShapeDtypeStruct((peers, gro...]
    broadcast_in_dim x1 -> x0, local copies, waits for them, and re-layouts: 0.74 us -> none  [forward(): hop1_count[:, None]]
  transfers between devices with their start and end apart: 8 -> 8, of which waited for: 2 -> 2; matrix products, arithmetic and copies ran while one was open for 2% -> 0% of each run, Pallas kernels for 17% -> 17%
where the time goes in v5:
time: 57.3 us; the launch traced here: 56.8 us
  Pallas kernels  28.4 us (50%)
  starting transfers between devices  19.2 us (34%)
  waiting for transfers between devices  9.14 us (16%)
    pallas_call x1, Pallas kernels, forward(): pl.pallas_call(functools.partial(finish_kernel, half, targets), out_shape...  11.7 us
    ppermute x3, waiting for transfers between devices, forward(): shards.append(lax.ppermute(hot_cache, 'gx', swaps[g]))  9.12 us
    ppermute x3, starting transfers between devices, forward(): colds[g] = lax.ppermute(colds[g], 'gx', swaps[g])  5.71 us
    pallas_call x1, Pallas kernels, forward(): pl.pallas_call(rank_kernel, out_shape=(jax.ShapeDtypeStruct((owners * lin...  5.33 us
    all_to_all x1, starting transfers between devices, forward(): lax.all_to_all(ask, 'gx', split_axis=0, concat_axis=0, axis_index_groups=...  5.21 us
    pallas_call x1, Pallas kernels, forward(): pl.pallas_call(functools.partial(remap_kernel, peers, owners, cold_rows,...  5.1 us
    pallas_call x1, Pallas kernels, forward(): pl.pallas_call(plan_kernel, out_shape=(jax.ShapeDtypeStruct((step,), jnp....  4.8 us
    ppermute x3, starting transfers between devices, forward(): shards.append(lax.ppermute(hot_cache, 'gx', swaps[g]))  4.45 us
  transfers between devices with their start and end apart: 8, of which 2 were waited for; matrix products, arithmetic and copies ran while one was open for 0% of the time, Pallas kernels for 17%

profile of v5, /device:TPU:0, one launch (start us, length us, event | category | flops | bytes accessed | tf_op | source)
XLA Modules:
  0.0 56.8 jit_solution(254464535065637277)
XLA Ops:
  0.0 0.0 copy-start
  0.0 5.3 %rank.1 = (f32[128,128]{1,0:T(8,128)}, bf16[8,144,128]{2,1,0:T(8,128)(2,1)}) custom-call(s32[11,128]{1,0:T(8,128)} %bitcast.13, s32[11,15,128]{2,1,0:T(8,128)} %bitcast.10, s32[1,32,32]{2,1,0:T(8,128)} %wanted.1, s32[1,32]{1,0:T(1,128)} %live.1, bf16[8192,128]{1,0:T(8,128)(2,1)} %table.1), custom_call_target="tpu_custom_call" | custom-call | tf_op jit(solution)/shard_map/rank/pallas_call | solution.py:311
  5.3 5.2 %all-to-all-start = ((bf16[8,144,128]{2,1,0:T(8,128)(2,1)}), bf16[8,144,128]{2,1,0:T(8,128)(2,1)S(1)}, u32[]{:S(2)}, u32[]{:S(2)}) async-start(bf16[8,144,128]{2,1,0:T(8,128)(2,1)} %get-tuple-element.25), calls=%async_computation | async-start | bytes 589824 | tf_op jit(solution)/shard_map/all_to_all | solution.py:328
  10.6 0.0 copy-done
  10.6 2.7 %collective-permute-start.1 = (bf16[512,128]{1,0:T(8,128)(2,1)S(1)}, bf16[512,128]{1,0:T(8,128)(2,1)S(1)}, u32[]{:S(2)}, u32[]{:S(2)}) collective-permute-start(bf16[512,128]{1,0:T(8,128)(2,1)S(1)} %copy-done), channel_id=1, source_target_pairs={{0,16},{1,17},{2,18},{3,19},{4,20},{5,21},{6,22},{7,23},{8,24},{9,... | collective-permute-start | bytes 393224 | tf_op jit(solution)/shard_map/ppermute | solution.py:310
  13.2 1.6 %collective-permute-start = (bf16[512,128]{1,0:T(8,128)(2,1)S(1)}, bf16[512,128]{1,0:T(8,128)(2,1)S(1)}, u32[]{:S(2)}, u32[]{:S(2)}) collective-permute-start(bf16[512,128]{1,0:T(8,128)(2,1)S(1)} %copy-done), channel_id=1, source_target_pairs={{0,8},{1,9},{2,10},{3,11},{4,12},{5,13},{6,14},{7,15},{8,0},{9,1},... | collective-permute-start | bytes 393224 | tf_op jit(solution)/shard_map/ppermute | solution.py:310
  14.8 0.2 collective-permute-start.2
  15.0 5.7 %collective-permute-done.1.refs_2_ = bf16[512,128]{1,0:T(8,128)(2,1)S(1)} collective-permute-done((bf16[512,128]{1,0:T(8,128)(2,1)S(1)}, bf16[512,128]{1,0:T(8,128)(2,1)S(1)}, u32[]{:S(2)}, u32[]{:S(2)}) %collective-permute-start.1) | collective-permute-done | bytes 131104 | tf_op jit(solution)/shard_map/ppermute | solution.py:310
  20.7 0.0 collective-permute-done.refs_1_
  20.7 3.4 %collective-permute-done.2.refs_3_ = bf16[512,128]{1,0:T(8,128)(2,1)S(1)} collective-permute-done((bf16[512,128]{1,0:T(8,128)(2,1)S(1)}, bf16[512,128]{1,0:T(8,128)(2,1)S(1)}, u32[]{:S(2)}, u32[]{:S(2)}) %collective-permute-start.2) | collective-permute-done | bytes 131104 | tf_op jit(solution)/shard_map/ppermute | solution.py:310
  24.1 0.0 all-to-all-done.asked
  24.1 1.5 %select.1 = (bf16[8,256,128]{2,1,0:T(8,128)(2,1)}, bf16[256,128]{1,0:T(8,128)(2,1)}, bf16[256,128]{1,0:T(8,128)(2,1)}, bf16[256,128]{1,0:T(8,128)(2,1)}, bf16[256,128]{1,0:T(8,128)(2,1)}) custom-call(bf16[8,144,128]{2,1,0:T(8,128)(2,1)S(1)} %all-to-all-done.asked, bf16[512,128]{1,0:T(8,128)(2,1)S(1)} %copy-done, ...), custom_call_target="tpu_custom_call" | custom-call | tf_op jit(solution)/shard_map/select/pallas_call | solution.py:331
  25.6 3.8 %all-to-all-start.1 = ((bf16[8,256,128]{2,1,0:T(8,128)(2,1)}), bf16[8,256,128]{2,1,0:T(8,128)(2,1)S(1)}, u32[]{:S(2)}, u32[]{:S(2)}) async-start(bf16[8,256,128]{2,1,0:T(8,128)(2,1)} %get-tuple-element.26), calls=%async_computation.1 | async-start | bytes 1048576 | tf_op jit(solution)/shard_map/all_to_all | solution.py:339
  29.5 2.3 %collective-permute-start.3 = (bf16[256,128]{1,0:T(8,128)(2,1)}, bf16[256,128]{1,0:T(8,128)(2,1)S(1)}, u32[]{:S(2)}, u32[]{:S(2)}) collective-permute-start(bf16[256,128]{1,0:T(8,128)(2,1)} %get-tuple-element.28), channel_id=1, source_target_pairs={{0,8},{1,9},{2,10},{3,11},{4,12},{5,13},{6,14},{7,15},{8,0},{9,1},... | collective-permute-start | bytes 196616 | tf_op jit(solution)/shard_map/ppermute | solution.py:343
  31.8 2.0 %collective-permute-start.4 = (bf16[256,128]{1,0:T(8,128)(2,1)}, bf16[256,128]{1,0:T(8,128)(2,1)S(1)}, u32[]{:S(2)}, u32[]{:S(2)}) collective-permute-start(bf16[256,128]{1,0:T(8,128)(2,1)} %get-tuple-element.29), channel_id=1, source_target_pairs={{0,16},{1,17},{2,18},{3,19},{4,20},{5,21},{6,22},{7,23},{8,24},{9,... | collective-permute-start | bytes 196616 | tf_op jit(solution)/shard_map/ppermute | solution.py:343
  33.8 1.4 %collective-permute-start.5 = (bf16[256,128]{1,0:T(8,128)(2,1)}, bf16[256,128]{1,0:T(8,128)(2,1)S(1)}, u32[]{:S(2)}, u32[]{:S(2)}) collective-permute-start(bf16[256,128]{1,0:T(8,128)(2,1)} %get-tuple-element.30), channel_id=1, source_target_pairs={{0,24},{1,25},{2,26},{3,27},{4,28},{5,29},{6,30},{7,31},{8,16},{9,... | collective-permute-start | bytes 196616 | tf_op jit(solution)/shard_map/ppermute | solution.py:343
  35.2 5.1 %remap.1 = (s32[192,128]{1,0:T(8,128)}, s32[11,128]{1,0:T(8,128)}, f32[128,128]{1,0:T(8,128)}) custom-call(s32[11,128]{1,0:T(8,128)} %bitcast.14, s32[11,15,128]{2,1,0:T(8,128)} %bitcast.11, s32[11,128]{1,0:T(8,128)} %bitcast.16, s32[1,128]{1,0:T(1,128)} %bitcast.17, f32[128,128]{1,0:T(8,128)} %get-tuple-element.18.rank), custom_call_target="tpu_custom_call" | custom-call | tf_op jit(solution)/shard_map/remap/pallas_call | solution.py:345
  40.3 4.8 %plan.1 = (s32[1536]{0:T(1024)}, s32[1536]{0:T(1024)}, s32[2]{0:T(128)}) custom-call(s32[128]{0:T(128)} %hop1.1, s32[1408]{0:T(1024)} %bitcast.15), custom_call_target="tpu_custom_call" | custom-call | tf_op jit(solution)/shard_map/plan/pallas_call | solution.py:356
  45.1 0.0 collective-permute-done.3.refs_2_
  45.1 0.0 collective-permute-done.4.refs_3_
  45.1 0.0 collective-permute-done.5.refs_4_
  45.1 0.0 all-to-all-done.1
  45.1 11.7 %finish.1 = f32[128,256]{1,0:T(8,128)} custom-call(s32[24576]{0:T(1024)} %bitcast.12, s32[1536]{0:T(1024)} %get-tuple-element.21.first, s32[1536]{0:T(1024)} %get-tuple-element.22.second, s32[2]{0:T(128)} %get-tuple-element.23.sizes, f32[128,128]{1,0:T(8,128)} %get-tuple-element.24.counts, bf16[256,256]{1,0:T(8,128)(2,1)} %w_first_in.1, f32[1,256]{1,0:T(1,128)} %bitcast.18, ...), custom_call_target="tpu_custom_call" | custom-call | tf_op jit(solution)/shard_map/finish/pallas_call | solution.py:369
Async XLA Ops:
  0.0 10.6 %copy-start = (bf16[512,128]{1,0:T(8,128)(2,1)S(1)}, bf16[512,128]{1,0:T(8,128)(2,1)}, u32[]{:S(2)}) copy-start(bf16[512,128]{1,0:T(8,128)(2,1)} %refs_0_.1) | copy-start | bytes 393220
  5.3 18.8 %all-to-all-start = ((bf16[8,144,128]{2,1,0:T(8,128)(2,1)}), bf16[8,144,128]{2,1,0:T(8,128)(2,1)S(1)}, u32[]{:S(2)}, u32[]{:S(2)}) async-start(bf16[8,144,128]{2,1,0:T(8,128)(2,1)} %get-tuple-element.25), calls=%async_computation | async-start | bytes 589824 | tf_op jit(solution)/shard_map/all_to_all | solution.py:328
  10.6 10.2 %collective-permute-start.1 = (bf16[512,128]{1,0:T(8,128)(2,1)S(1)}, bf16[512,128]{1,0:T(8,128)(2,1)S(1)}, u32[]{:S(2)}, u32[]{:S(2)}) collective-permute-start(bf16[512,128]{1,0:T(8,128)(2,1)S(1)} %copy-done), channel_id=1, source_target_pairs={{0,16},{1,17},{2,18},{3,19},{4,20},{5,21},{6,22},{7,23},{8,24},{9,... | collective-permute-start | bytes 393224 | tf_op jit(solution)/shard_map/ppermute | solution.py:310
  13.2 7.5 %collective-permute-start = (bf16[512,128]{1,0:T(8,128)(2,1)S(1)}, bf16[512,128]{1,0:T(8,128)(2,1)S(1)}, u32[]{:S(2)}, u32[]{:S(2)}) collective-permute-start(bf16[512,128]{1,0:T(8,128)(2,1)S(1)} %copy-done), channel_id=1, source_target_pairs={{0,8},{1,9},{2,10},{3,11},{4,12},{5,13},{6,14},{7,15},{8,0},{9,1},... | collective-permute-start | bytes 393224 | tf_op jit(solution)/shard_map/ppermute | solution.py:310
  14.8 9.3 %collective-permute-start.2 = (bf16[512,128]{1,0:T(8,128)(2,1)S(1)}, bf16[512,128]{1,0:T(8,128)(2,1)S(1)}, u32[]{:S(2)}, u32[]{:S(2)}) collective-permute-start(bf16[512,128]{1,0:T(8,128)(2,1)S(1)} %copy-done), channel_id=1, source_target_pairs={{0,24},{1,25},{2,26},{3,27},{4,28},{5,29},{6,30},{7,31},{8,16},{9,... | collective-permute-start | bytes 393224 | tf_op jit(solution)/shard_map/ppermute | solution.py:310
  25.6 19.5 %all-to-all-start.1 = ((bf16[8,256,128]{2,1,0:T(8,128)(2,1)}), bf16[8,256,128]{2,1,0:T(8,128)(2,1)S(1)}, u32[]{:S(2)}, u32[]{:S(2)}) async-start(bf16[8,256,128]{2,1,0:T(8,128)(2,1)} %get-tuple-element.26), calls=%async_computation.1 | async-start | bytes 1048576 | tf_op jit(solution)/shard_map/all_to_all | solution.py:339
  29.5 15.6 %collective-permute-start.3 = (bf16[256,128]{1,0:T(8,128)(2,1)}, bf16[256,128]{1,0:T(8,128)(2,1)S(1)}, u32[]{:S(2)}, u32[]{:S(2)}) collective-permute-start(bf16[256,128]{1,0:T(8,128)(2,1)} %get-tuple-element.28), channel_id=1, source_target_pairs={{0,8},{1,9},{2,10},{3,11},{4,12},{5,13},{6,14},{7,15},{8,0},{9,1},... | collective-permute-start | bytes 196616 | tf_op jit(solution)/shard_map/ppermute | solution.py:343
  31.8 13.3 %collective-permute-start.4 = (bf16[256,128]{1,0:T(8,128)(2,1)}, bf16[256,128]{1,0:T(8,128)(2,1)S(1)}, u32[]{:S(2)}, u32[]{:S(2)}) collective-permute-start(bf16[256,128]{1,0:T(8,128)(2,1)} %get-tuple-element.29), channel_id=1, source_target_pairs={{0,16},{1,17},{2,18},{3,19},{4,20},{5,21},{6,22},{7,23},{8,24},{9,... | collective-permute-start | bytes 196616 | tf_op jit(solution)/shard_map/ppermute | solution.py:343
  33.8 11.3 %collective-permute-start.5 = (bf16[256,128]{1,0:T(8,128)(2,1)}, bf16[256,128]{1,0:T(8,128)(2,1)S(1)}, u32[]{:S(2)}, u32[]{:S(2)}) collective-permute-start(bf16[256,128]{1,0:T(8,128)(2,1)} %get-tuple-element.30), channel_id=1, source_target_pairs={{0,24},{1,25},{2,26},{3,27},{4,28},{5,29},{6,30},{7,31},{8,16},{9,... | collective-permute-start | bytes 196616 | tf_op jit(solution)/shard_map/ppermute | solution.py:343

commit v6 on v5

--- a/solution.py
+++ b/solution.py
@@ -36,7 +36,10 @@
     return jnp.where(iota == wide, one, zero)
 
 
-def rank_kernel(own, near, wanted, live, table, rank, ask, held, wide, raw, stage, sems):
+def rank_kernel(
+    own, near, wanted_in, live_in, table, rank_out, ask_out,
+    rank, ask, held, wide, raw, stage, wanted, live, sems, sent,
+):
     pieces = sems.shape[0]
     size = table.shape[0] // pieces
     copies = [
@@ -45,7 +48,11 @@
         )
         for i in range(pieces)
     ]
-    for copy in copies:
+    lists = [
+        pltpu.make_async_copy(source, target, sent.at[i])
+        for i, (source, target) in enumerate(((wanted_in, wanted), (live_in, live)))
+    ]
+    for copy in lists + copies:
         copy.start()
     peers, groups = ask.shape[0], held.shape[0] // ask.shape[0]
     high = rank.shape[0]
@@ -75,6 +82,8 @@
     offset = jnp.dot(earlier, sums, preferred_element_type=jnp.float32)
     value = jnp.where(used, inside + offset, -1.0)
     rank[...] = value
+    ranks_sent = pltpu.make_async_copy(rank, rank_out, sent.at[ask.shape[0]])
+    ranks_sent.start()
     held[...] = value.reshape(held.shape)
     here = lax.axis_index("gx") // peers
     for p in range(peers):
@@ -82,31 +91,44 @@
             [held[(here ^ g) * peers + p] for g in range(groups)], 0
         ).astype(ask.dtype)
 
+    for copy in lists:
+        copy.wait()
     for i, copy in enumerate(copies):
         copy.wait()
         part = pl.ds(i * size, size)
         wide[part, :] = raw[part, :].astype(jnp.float32)
     cold_rows = stage.shape[0]
     line = lax.broadcasted_iota(jnp.int32, stage.shape, 0)
-    for g in range(groups):
-        place = pl.ds(groups * lines + g * cold_rows, cold_rows)
-
-        def one_device(p, carry, g=g, place=place):
+    columns = [wanted.at[:, :, pl.ds(j, cold_rows - j)] for j in range(cold_rows)]
+
+    def one_device(p, carry):
+        for g in range(groups):
             d = (here ^ g) * peers + p
             for j in range(cold_rows):
-                stage[j : j + 1, :] = wide[pl.ds(wanted[0, d, j], 1), :]
+                stage[j : j + 1, :] = wide[pl.ds(columns[j][0, d, 0], 1), :]
+            place = pl.ds(groups * lines + g * cold_rows, cold_rows)
             ask[p, place, :] = jnp.where(line < live[0, d], stage[...], 0.0).astype(ask.dtype)
-            return carry
-
-        lax.fori_loop(0, peers, one_device, 0)
+        pltpu.make_async_copy(ask.at[p], ask_out.at[p], sent.at[p]).start()
+        return carry
+
+    lax.fori_loop(0, peers, one_device, 0)
+    for p in range(peers):
+        pltpu.make_async_copy(ask.at[p], ask_out.at[p], sent.at[p]).wait()
+    ranks_sent.wait()
 
 
 def select_kernel(asked, *refs):
-    groups = (len(refs) - 1) // 2
-    shards, out, colds = refs[:groups], refs[groups], refs[groups + 1 :]
+    groups = (len(refs) - 3) // 2
+    shards, out, colds = refs[:groups], refs[groups], refs[groups + 1 : -2]
+    held, sent = refs[-2:]
     peers = asked.shape[0]
     lines = shards[0].shape[0] // LANES
-    cold_rows = colds[0].shape[0] // peers
+    cold_rows = colds[0].shape[1]
+    copies = []
+    for g, cold in enumerate(colds):
+        place = pl.ds(groups * lines + g * cold_rows, cold_rows)
+        copies.append(pltpu.make_async_copy(asked.at[:, place], cold, sent.at[g]))
+        copies[-1].start()
     want = lax.broadcasted_iota(jnp.int32, (HOT_REQ, LANES), 0).astype(jnp.float32)
     ranks = [asked[p, 0 : groups * lines, :].astype(jnp.float32) for p in range(peers)]
     for g, shard in enumerate(shards):
@@ -121,12 +143,14 @@
         picked = jnp.dot(
             jnp.concatenate(picks, 0), shard[...], preferred_element_type=jnp.float32
         ).astype(out.dtype)
-        place = groups * lines + g * cold_rows
-        for p in range(peers):
-            out[p, g * HOT_REQ : (g + 1) * HOT_REQ, :] = picked[p * HOT_REQ : (p + 1) * HOT_REQ]
-            colds[g][p * cold_rows : (p + 1) * cold_rows, :] = asked[
-                p, place : place + cold_rows, :
-            ]
+        place = pl.ds(g * HOT_REQ, HOT_REQ)
+        held[:, place, :] = picked.reshape(peers, HOT_REQ, picked.shape[1])
+        copies.append(
+            pltpu.make_async_copy(held.at[:, place], out.at[:, place], sent.at[groups + g])
+        )
+        copies[-1].start()
+    for copy in copies:
+        copy.wait()
 
 
 def remap_kernel(peers, owners, cold_rows, half, own, near, count, ones, rank, out, place, sizes):
@@ -219,30 +243,37 @@
 
 
 def finish_kernel(
-    half, targets, slots_in, first, second, sizes, counts,
+    half, targets, slots_in, first_in, second_in, sizes_in, counts_in,
     w_first_in, b_first, w_second_in, b_second, *refs,
 ):
-    blocks = refs[:-9]
-    out, table, own, total, extra, slots, w_first, w_second, sems = refs[-9:]
-    width = own.shape[1]
+    blocks = refs[:-12]
+    out, table, kept, extra, slots, w_first, w_second, first, second, sizes, counts, sems = refs[
+        -12:
+    ]
+    step, width = extra.shape
+    own, total = kept.at[pl.ds(0, step)], kept.at[pl.ds(step, step)]
     seeds = counts.shape[0]
-    step = own.shape[0]
     per = slots.shape[0] // step
     copies = [
         pltpu.make_async_copy(slots_in.at[here], slots.at[here], sems.at[i])
         for i, here in enumerate((pl.ds(0, half * step), pl.ds(half * step, (per - half) * step)))
     ]
-    copies.append(pltpu.make_async_copy(w_first_in, w_first, sems.at[2]))
-    copies.append(pltpu.make_async_copy(w_second_in, w_second, sems.at[3]))
-    for copy in copies:
-        copy.start()
+    later = (
+        (w_first_in, w_first), (w_second_in, w_second), (first_in, first), (second_in, second),
+        (sizes_in, sizes), (counts_in, counts),
+    )
+    for i, (source, target) in enumerate(later):
+        copies.append(pltpu.make_async_copy(source, target, sems.at[2 + i]))
+    for i in (0, 4, 6, 5, 1, 2, 3, 7):
+        copies[i].start()
     n_rows = 0
     for block in blocks:
         table[pl.ds(n_rows, block.shape[0]), :] = block[...].astype(jnp.float32)
         n_rows += block.shape[0]
     table[pl.ds(n_rows, 8), :] = jnp.zeros((8, width), jnp.float32)
     extra[...] = jnp.zeros(extra.shape, jnp.float32)
-    copies[0].wait()
+    for i in (0, 4, 6, 5):
+        copies[i].wait()
 
     parts = [slots.at[pl.ds(k * step, step)] for k in range(per)]
 
@@ -267,6 +298,7 @@
     lax.fori_loop(0, sizes[1], second_part, 0)
     copies[2].wait()
     copies[3].wait()
+    copies[7].wait()
 
     pooled = jnp.zeros((seeds, w_first.shape[1]), jnp.float32)
     near = counts[:, targets : targets + 1]
@@ -314,14 +346,19 @@
             jax.ShapeDtypeStruct((owners * lines, LANES), jnp.float32),
             jax.ShapeDtypeStruct((peers, groups * (lines + cold_rows), width), jnp.bfloat16),
         ),
-        in_specs=[VMEM, VMEM, SMEM, SMEM, ANY],
-        out_specs=(VMEM, VMEM),
+        in_specs=[VMEM, VMEM, ANY, ANY, ANY],
+        out_specs=(ANY, ANY),
         scratch_shapes=[
+            pltpu.VMEM((owners * lines, LANES), jnp.float32),
+            pltpu.VMEM((peers, groups * (lines + cold_rows), width), jnp.bfloat16),
             pltpu.VMEM((owners, lines, LANES), jnp.float32),
             pltpu.VMEM(cold_table.shape, jnp.float32),
             pltpu.VMEM(cold_table.shape, cold_table.dtype),
             pltpu.VMEM((cold_rows, width), jnp.float32),
+            pltpu.SMEM(serve_index.shape, jnp.int32),
+            pltpu.SMEM(serve_count.shape, jnp.int32),
             pltpu.SemaphoreType.DMA((8,)),
+            pltpu.SemaphoreType.DMA((peers + 1,)),
         ],
         name="rank",
     )(own_slot, near_slot, serve_index, serve_count, cold_table)
@@ -331,9 +368,13 @@
     answer, *colds = pl.pallas_call(
         select_kernel,
         out_shape=[jax.ShapeDtypeStruct((peers, groups * HOT_REQ, width), hot_cache.dtype)]
-        + [jax.ShapeDtypeStruct((peers * cold_rows, width), hot_cache.dtype)] * groups,
+        + [jax.ShapeDtypeStruct((peers, cold_rows, width), hot_cache.dtype)] * groups,
         in_specs=[VMEM] * (1 + groups),
-        out_specs=[VMEM] * (1 + groups),
+        out_specs=[ANY] * (1 + groups),
+        scratch_shapes=[
+            pltpu.VMEM((peers, groups * HOT_REQ, width), hot_cache.dtype),
+            pltpu.SemaphoreType.DMA((2 * groups,)),
+        ],
         name="select",
     )(in_vmem(asked), in_vmem(hot_cache), *map(in_vmem, shards[1:]))
     received = lax.all_to_all(
@@ -369,23 +410,27 @@
     return pl.pallas_call(
         functools.partial(finish_kernel, half, targets),
         out_shape=jax.ShapeDtypeStruct((seeds, w_second.shape[1]), jnp.float32),
-        in_specs=[ANY] + [SMEM] * 3 + [VMEM] + [ANY, VMEM, ANY, VMEM] + [VMEM] * (1 + groups),
+        in_specs=[ANY] * 5 + [ANY, VMEM, ANY, VMEM] + [VMEM] * (1 + groups),
         out_specs=VMEM,
         scratch_shapes=[
             pltpu.VMEM((rows + 8, width), jnp.float32),
-            pltpu.VMEM((step, width), jnp.float32),
-            pltpu.VMEM((step, width), jnp.float32),
+            pltpu.VMEM((2 * step, width), jnp.float32),
             pltpu.VMEM((step, width), jnp.float32),
             pltpu.SMEM(((fan + 1) * step,), jnp.int32),
             pltpu.VMEM(w_first.shape, w_first.dtype),
             pltpu.VMEM(w_second.shape, w_second.dtype),
-            pltpu.SemaphoreType.DMA((4,)),
+            pltpu.SMEM((step,), jnp.int32),
+            pltpu.SMEM((step,), jnp.int32),
+            pltpu.SMEM((2,), jnp.int32),
+            pltpu.VMEM((seeds, LANES), jnp.float32),
+            pltpu.SemaphoreType.DMA((8,)),
         ],
         name="finish",
     )(
         slots.reshape(-1), first, second, sizes, counts,
         w_first, b_first[None], w_second, b_second[None],
-        in_vmem(received.reshape(owners * HOT_REQ, width)), colds[0], *map(in_vmem, colds[1:]),
+        in_vmem(received.reshape(owners * HOT_REQ, width)),
+        colds[0].reshape(-1, width), *(in_vmem(c.reshape(-1, width)) for c in colds[1:]),
     )
 
 

time: 57.3 us -> 56.8 us (level)
  transfers between devices with their start and end apart: 8 -> 8, of which waited for: 2 -> 2; matrix products, arithmetic and copies ran while one was open for 0% -> 0% of each run, Pallas kernels for 17% -> 18%
where the time goes in v6:
time: 56.8 us; the launch traced here: 56.3 us
  Pallas kernels  27.9 us (49%)
  starting transfers between devices  19.2 us (34%)
  waiting for transfers between devices  9.14 us (16%)
    pallas_call x1, Pallas kernels, forward(): pl.pallas_call(functools.partial(finish_kernel, half, targets), out_shape...  11.6 us
    ppermute x3, waiting for transfers between devices, forward(): shards.append(lax.ppermute(hot_cache, 'gx', swaps[g]))  9.13 us
    ppermute x3, starting transfers between devices, forward(): colds[g] = lax.ppermute(colds[g], 'gx', swaps[g])  5.71 us
    all_to_all x1, starting transfers between devices, forward(): lax.all_to_all(ask, 'gx', split_axis=0, concat_axis=0, axis_index_groups=...  5.21 us
    pallas_call x1, Pallas kernels, forward(): pl.pallas_call(functools.partial(remap_kernel, peers, owners, cold_rows,...  5.1 us
    pallas_call x1, Pallas kernels, forward(): pl.pallas_call(rank_kernel, out_shape=(jax.ShapeDtypeStruct((owners * lin...  4.82 us
    pallas_call x1, Pallas kernels, forward(): pl.pallas_call(plan_kernel, out_shape=(jax.ShapeDtypeStruct((step,), jnp....  4.8 us
    ppermute x3, starting transfers between devices, forward(): shards.append(lax.ppermute(hot_cache, 'gx', swaps[g]))  4.45 us
  transfers between devices with their start and end apart: 8, of which 2 were waited for; matrix products, arithmetic and copies ran while one was open for 0% of the time, Pallas kernels for 18%

profile of v6, /device:TPU:0, one launch (start us, length us, event | category | flops | bytes accessed | tf_op | source)
XLA Modules:
  0.0 56.3 jit_solution(574287093050486455)
XLA Ops:
  0.0 0.0 copy-start
  0.0 4.8 %rank.1 = (f32[128,128]{1,0:T(8,128)}, bf16[8,144,128]{2,1,0:T(8,128)(2,1)}) custom-call(s32[11,128]{1,0:T(8,128)} %bitcast.21, s32[11,15,128]{2,1,0:T(8,128)} %bitcast.17, s32[1,32,32]{2,1,0:T(8,128)} %wanted_in.1, s32[1,32]{1,0:T(1,128)} %live_in.1, bf16[8192,128]{1,0:T(8,128)(2,1)} %table.1), custom_call_target="tpu_custom_call" | custom-call | tf_op jit(solution)/shard_map/rank/pallas_call | solution.py:343
  4.8 5.2 %all-to-all-start = ((bf16[8,144,128]{2,1,0:T(8,128)(2,1)}), bf16[8,144,128]{2,1,0:T(8,128)(2,1)S(1)}, u32[]{:S(2)}, u32[]{:S(2)}) async-start(bf16[8,144,128]{2,1,0:T(8,128)(2,1)} %get-tuple-element.25), calls=%async_computation | async-start | bytes 589824 | tf_op jit(solution)/shard_map/all_to_all | solution.py:365
  10.0 0.0 copy-done
  10.0 2.7 %collective-permute-start.1 = (bf16[512,128]{1,0:T(8,128)(2,1)S(1)}, bf16[512,128]{1,0:T(8,128)(2,1)S(1)}, u32[]{:S(2)}, u32[]{:S(2)}) collective-permute-start(bf16[512,128]{1,0:T(8,128)(2,1)S(1)} %copy-done), channel_id=1, source_target_pairs={{0,16},{1,17},{2,18},{3,19},{4,20},{5,21},{6,22},{7,23},{8,24},{9,... | collective-permute-start | bytes 393224 | tf_op jit(solution)/shard_map/ppermute | solution.py:342
  12.7 1.6 %collective-permute-start = (bf16[512,128]{1,0:T(8,128)(2,1)S(1)}, bf16[512,128]{1,0:T(8,128)(2,1)S(1)}, u32[]{:S(2)}, u32[]{:S(2)}) collective-permute-start(bf16[512,128]{1,0:T(8,128)(2,1)S(1)} %copy-done), channel_id=1, source_target_pairs={{0,8},{1,9},{2,10},{3,11},{4,12},{5,13},{6,14},{7,15},{8,0},{9,1},... | collective-permute-start | bytes 393224 | tf_op jit(solution)/shard_map/ppermute | solution.py:342
  14.3 0.2 collective-permute-start.2
  14.5 5.7 %collective-permute-done.1.refs_2_ = bf16[512,128]{1,0:T(8,128)(2,1)S(1)} collective-permute-done((bf16[512,128]{1,0:T(8,128)(2,1)S(1)}, bf16[512,128]{1,0:T(8,128)(2,1)S(1)}, u32[]{:S(2)}, u32[]{:S(2)}) %collective-permute-start.1) | collective-permute-done | bytes 131104 | tf_op jit(solution)/shard_map/ppermute | solution.py:342
  20.2 0.0 collective-permute-done.refs_1_
  20.2 3.4 %collective-permute-done.2.refs_3_ = bf16[512,128]{1,0:T(8,128)(2,1)S(1)} collective-permute-done((bf16[512,128]{1,0:T(8,128)(2,1)S(1)}, bf16[512,128]{1,0:T(8,128)(2,1)S(1)}, u32[]{:S(2)}, u32[]{:S(2)}) %collective-permute-start.2) | collective-permute-done | bytes 131104 | tf_op jit(solution)/shard_map/ppermute | solution.py:342
  23.6 0.0 all-to-all-done.asked
  23.6 1.5 %select.1 = (bf16[8,256,128]{2,1,0:T(8,128)(2,1)}, bf16[8,32,128]{2,1,0:T(8,128)(2,1)}, bf16[8,32,128]{2,1,0:T(8,128)(2,1)}, bf16[8,32,128]{2,1,0:T(8,128)(2,1)}, bf16[8,32,128]{2,1,0:T(8,128)(2,1)}) custom-call(bf16[8,144,128]{2,1,0:T(8,128)(2,1)S(1)} %all-to-all-done.asked, bf16[512,128]{1,0:T(8,128)(2,1)S(1)} %copy-done, ...), custom_call_target="tpu_custom_call" | custom-call | tf_op jit(solution)/shard_map/select/pallas_call | solution.py:368
  25.2 3.8 %all-to-all-start.1 = ((bf16[8,256,128]{2,1,0:T(8,128)(2,1)}), bf16[8,256,128]{2,1,0:T(8,128)(2,1)S(1)}, u32[]{:S(2)}, u32[]{:S(2)}) async-start(bf16[8,256,128]{2,1,0:T(8,128)(2,1)} %get-tuple-element.26), calls=%async_computation.1 | async-start | bytes 1048576 | tf_op jit(solution)/shard_map/all_to_all | solution.py:380
  29.0 2.3 %collective-permute-start.3 = (bf16[8,32,128]{2,1,0:T(8,128)(2,1)}, bf16[8,32,128]{2,1,0:T(8,128)(2,1)S(1)}, u32[]{:S(2)}, u32[]{:S(2)}) collective-permute-start(bf16[8,32,128]{2,1,0:T(8,128)(2,1)} %get-tuple-element.28), channel_id=1, source_target_pairs={{0,8},{1,9},{2,10},{3,11},{4,12},{5,13},{6,14},{7,15},{8,0},{9,1},... | collective-permute-start | bytes 196616 | tf_op jit(solution)/shard_map/ppermute | solution.py:384
  31.3 2.0 %collective-permute-start.4 = (bf16[8,32,128]{2,1,0:T(8,128)(2,1)}, bf16[8,32,128]{2,1,0:T(8,128)(2,1)S(1)}, u32[]{:S(2)}, u32[]{:S(2)}) collective-permute-start(bf16[8,32,128]{2,1,0:T(8,128)(2,1)} %get-tuple-element.29), channel_id=1, source_target_pairs={{0,16},{1,17},{2,18},{3,19},{4,20},{5,21},{6,22},{7,23},{8,24},{9,... | collective-permute-start | bytes 196616 | tf_op jit(solution)/shard_map/ppermute | solution.py:384
  33.3 1.4 %collective-permute-start.5 = (bf16[8,32,128]{2,1,0:T(8,128)(2,1)}, bf16[8,32,128]{2,1,0:T(8,128)(2,1)S(1)}, u32[]{:S(2)}, u32[]{:S(2)}) collective-permute-start(bf16[8,32,128]{2,1,0:T(8,128)(2,1)} %get-tuple-element.30), channel_id=1, source_target_pairs={{0,24},{1,25},{2,26},{3,27},{4,28},{5,29},{6,30},{7,31},{8,16},{9,... | collective-permute-start | bytes 196616 | tf_op jit(solution)/shard_map/ppermute | solution.py:384
  34.7 5.1 %remap.1 = (s32[192,128]{1,0:T(8,128)}, s32[11,128]{1,0:T(8,128)}, f32[128,128]{1,0:T(8,128)}) custom-call(s32[11,128]{1,0:T(8,128)} %bitcast.22, s32[11,15,128]{2,1,0:T(8,128)} %bitcast.18, s32[11,128]{1,0:T(8,128)} %bitcast.24, s32[1,128]{1,0:T(1,128)} %bitcast.25, f32[128,128]{1,0:T(8,128)} %get-tuple-element.18.rank), custom_call_target="tpu_custom_call" | custom-call | tf_op jit(solution)/shard_map/remap/pallas_call | solution.py:386
  39.8 4.8 %plan.1 = (s32[1536]{0:T(1024)}, s32[1536]{0:T(1024)}, s32[2]{0:T(128)}) custom-call(s32[128]{0:T(128)} %hop1.1, s32[1408]{0:T(1024)} %bitcast.23), custom_call_target="tpu_custom_call" | custom-call | tf_op jit(solution)/shard_map/plan/pallas_call | solution.py:397
  44.6 0.0 collective-permute-done.3
  44.6 0.0 collective-permute-done.4
  44.6 0.0 collective-permute-done.5
  44.6 0.0 all-to-all-done.1
  44.6 11.6 %finish.1 = f32[128,256]{1,0:T(8,128)} custom-call(s32[24576]{0:T(1024)} %bitcast.19, s32[1536]{0:T(1024)} %get-tuple-element.21.first_in, s32[1536]{0:T(1024)} %get-tuple-element.22.second_in, s32[2]{0:T(128)} %get-tuple-element.23.sizes_in, f32[128,128]{1,0:T(8,128)} %get-tuple-element.24.counts_in, bf16[256,256]{1,0:T(8,128)(2,1)} %w_first_in.1, ...), custom_call_target="tpu_custom_call" | custom-call | tf_op jit(solution)/shard_map/finish/pallas_call | solution.py:410
Async XLA Ops:
  0.0 10.0 %copy-start = (bf16[512,128]{1,0:T(8,128)(2,1)S(1)}, bf16[512,128]{1,0:T(8,128)(2,1)}, u32[]{:S(2)}) copy-start(bf16[512,128]{1,0:T(8,128)(2,1)} %refs_0_.1) | copy-start | bytes 393220
  4.8 18.8 %all-to-all-start = ((bf16[8,144,128]{2,1,0:T(8,128)(2,1)}), bf16[8,144,128]{2,1,0:T(8,128)(2,1)S(1)}, u32[]{:S(2)}, u32[]{:S(2)}) async-start(bf16[8,144,128]{2,1,0:T(8,128)(2,1)} %get-tuple-element.25), calls=%async_computation | async-start | bytes 589824 | tf_op jit(solution)/shard_map/all_to_all | solution.py:365
  10.0 10.1 %collective-permute-start.1 = (bf16[512,128]{1,0:T(8,128)(2,1)S(1)}, bf16[512,128]{1,0:T(8,128)(2,1)S(1)}, u32[]{:S(2)}, u32[]{:S(2)}) collective-permute-start(bf16[512,128]{1,0:T(8,128)(2,1)S(1)} %copy-done), channel_id=1, source_target_pairs={{0,16},{1,17},{2,18},{3,19},{4,20},{5,21},{6,22},{7,23},{8,24},{9,... | collective-permute-start | bytes 393224 | tf_op jit(solution)/shard_map/ppermute | solution.py:342
  12.7 7.5 %collective-permute-start = (bf16[512,128]{1,0:T(8,128)(2,1)S(1)}, bf16[512,128]{1,0:T(8,128)(2,1)S(1)}, u32[]{:S(2)}, u32[]{:S(2)}) collective-permute-start(bf16[512,128]{1,0:T(8,128)(2,1)S(1)} %copy-done), channel_id=1, source_target_pairs={{0,8},{1,9},{2,10},{3,11},{4,12},{5,13},{6,14},{7,15},{8,0},{9,1},... | collective-permute-start | bytes 393224 | tf_op jit(solution)/shard_map/ppermute | solution.py:342
  14.3 9.4 %collective-permute-start.2 = (bf16[512,128]{1,0:T(8,128)(2,1)S(1)}, bf16[512,128]{1,0:T(8,128)(2,1)S(1)}, u32[]{:S(2)}, u32[]{:S(2)}) collective-permute-start(bf16[512,128]{1,0:T(8,128)(2,1)S(1)} %copy-done), channel_id=1, source_target_pairs={{0,24},{1,25},{2,26},{3,27},{4,28},{5,29},{6,30},{7,31},{8,16},{9,... | collective-permute-start | bytes 393224 | tf_op jit(solution)/shard_map/ppermute | solution.py:342
  25.2 19.5 %all-to-all-start.1 = ((bf16[8,256,128]{2,1,0:T(8,128)(2,1)}), bf16[8,256,128]{2,1,0:T(8,128)(2,1)S(1)}, u32[]{:S(2)}, u32[]{:S(2)}) async-start(bf16[8,256,128]{2,1,0:T(8,128)(2,1)} %get-tuple-element.26), calls=%async_computation.1 | async-start | bytes 1048576 | tf_op jit(solution)/shard_map/all_to_all | solution.py:380
  29.0 15.6 %collective-permute-start.3 = (bf16[8,32,128]{2,1,0:T(8,128)(2,1)}, bf16[8,32,128]{2,1,0:T(8,128)(2,1)S(1)}, u32[]{:S(2)}, u32[]{:S(2)}) collective-permute-start(bf16[8,32,128]{2,1,0:T(8,128)(2,1)} %get-tuple-element.28), channel_id=1, source_target_pairs={{0,8},{1,9},{2,10},{3,11},{4,12},{5,13},{6,14},{7,15},{8,0},{9,1},... | collective-permute-start | bytes 196616 | tf_op jit(solution)/shard_map/ppermute | solution.py:384
  31.3 13.3 %collective-permute-start.4 = (bf16[8,32,128]{2,1,0:T(8,128)(2,1)}, bf16[8,32,128]{2,1,0:T(8,128)(2,1)S(1)}, u32[]{:S(2)}, u32[]{:S(2)}) collective-permute-start(bf16[8,32,128]{2,1,0:T(8,128)(2,1)} %get-tuple-element.29), channel_id=1, source_target_pairs={{0,16},{1,17},{2,18},{3,19},{4,20},{5,21},{6,22},{7,23},{8,24},{9,... | collective-permute-start | bytes 196616 | tf_op jit(solution)/shard_map/ppermute | solution.py:384
  33.3 11.3 %collective-permute-start.5 = (bf16[8,32,128]{2,1,0:T(8,128)(2,1)}, bf16[8,32,128]{2,1,0:T(8,128)(2,1)S(1)}, u32[]{:S(2)}, u32[]{:S(2)}) collective-permute-start(bf16[8,32,128]{2,1,0:T(8,128)(2,1)} %get-tuple-element.30), channel_id=1, source_target_pairs={{0,24},{1,25},{2,26},{3,27},{4,28},{5,29},{6,30},{7,31},{8,16},{9,... | collective-permute-start | bytes 196616 | tf_op jit(solution)/shard_map/ppermute | solution.py:384

commit v7 on v6

--- a/solution.py
+++ b/solution.py
@@ -11,7 +11,7 @@
 LANES = 128
 HOT_REQ = 64
 PEERS = 8
-TASKS = 32
+TASKS = 24
 
 VMEM = pl.BlockSpec(memory_space=pltpu.VMEM)
 SMEM = pl.BlockSpec(memory_space=pltpu.SMEM)
@@ -37,8 +37,8 @@
 
 
 def rank_kernel(
-    own, near, wanted_in, live_in, table, rank_out, ask_out,
-    rank, ask, held, wide, raw, stage, wanted, live, sems, sent,
+    own_in, near_in, wanted_in, live_in, table, rank_out, ask_out,
+    rank, ask, held, wide, raw, stage, own, near, wanted, live, sems, sent,
 ):
     pieces = sems.shape[0]
     size = table.shape[0] // pieces
@@ -50,10 +50,14 @@
     ]
     lists = [
         pltpu.make_async_copy(source, target, sent.at[i])
-        for i, (source, target) in enumerate(((wanted_in, wanted), (live_in, live)))
+        for i, (source, target) in enumerate(
+            ((near_in, near), (own_in, own), (wanted_in, wanted), (live_in, live))
+        )
     ]
     for copy in lists + copies:
         copy.start()
+    lists[0].wait()
+    lists[1].wait()
     peers, groups = ask.shape[0], held.shape[0] // ask.shape[0]
     high = rank.shape[0]
     lines = high // held.shape[0]
@@ -91,7 +95,7 @@
             [held[(here ^ g) * peers + p] for g in range(groups)], 0
         ).astype(ask.dtype)
 
-    for copy in lists:
+    for copy in lists[2:]:
         copy.wait()
     for i, copy in enumerate(copies):
         copy.wait()
@@ -244,34 +248,38 @@
 
 def finish_kernel(
     half, targets, slots_in, first_in, second_in, sizes_in, counts_in,
-    w_first_in, b_first, w_second_in, b_second, *refs,
+    w_first_in, b_first_in, w_second_in, b_second_in, here_in, *refs,
 ):
-    blocks = refs[:-12]
-    out, table, kept, extra, slots, w_first, w_second, first, second, sizes, counts, sems = refs[
-        -12:
-    ]
+    (
+        out, table, kept, extra, slots, w_first, w_second, first, second, sizes, counts,
+        b_first, b_second, here, sems,
+    ) = refs[-15:]
+    blocks = (refs[0], here, *refs[1:-15])
     step, width = extra.shape
     own, total = kept.at[pl.ds(0, step)], kept.at[pl.ds(step, step)]
     seeds = counts.shape[0]
     per = slots.shape[0] // step
     copies = [
-        pltpu.make_async_copy(slots_in.at[here], slots.at[here], sems.at[i])
-        for i, here in enumerate((pl.ds(0, half * step), pl.ds(half * step, (per - half) * step)))
+        pltpu.make_async_copy(slots_in.at[part], slots.at[part], sems.at[i])
+        for i, part in enumerate((pl.ds(0, half * step), pl.ds(half * step, (per - half) * step)))
     ]
     later = (
         (w_first_in, w_first), (w_second_in, w_second), (first_in, first), (second_in, second),
-        (sizes_in, sizes), (counts_in, counts),
+        (sizes_in, sizes), (counts_in, counts), (b_first_in, b_first), (b_second_in, b_second),
+        (here_in, here),
     )
     for i, (source, target) in enumerate(later):
         copies.append(pltpu.make_async_copy(source, target, sems.at[2 + i]))
-    for i in (0, 4, 6, 5, 1, 2, 3, 7):
+    for i in (0, 4, 6, 10, 5, 1, 2, 3, 7, 8, 9):
         copies[i].start()
+    extra[...] = jnp.zeros(extra.shape, jnp.float32)
     n_rows = 0
     for block in blocks:
+        if block is here:
+            copies[10].wait()
         table[pl.ds(n_rows, block.shape[0]), :] = block[...].astype(jnp.float32)
         n_rows += block.shape[0]
     table[pl.ds(n_rows, 8), :] = jnp.zeros((8, width), jnp.float32)
-    extra[...] = jnp.zeros(extra.shape, jnp.float32)
     for i in (0, 4, 6, 5):
         copies[i].wait()
 
@@ -296,9 +304,8 @@
     lax.fori_loop(0, sizes[0], first_part, 0)
     copies[1].wait()
     lax.fori_loop(0, sizes[1], second_part, 0)
-    copies[2].wait()
-    copies[3].wait()
-    copies[7].wait()
+    for i in (2, 3, 7, 8, 9):
+        copies[i].wait()
 
     pooled = jnp.zeros((seeds, w_first.shape[1]), jnp.float32)
     near = counts[:, targets : targets + 1]
@@ -330,7 +337,7 @@
     groups = owners // peers
     teams = [[g * peers + p for p in range(peers)] for g in range(groups)]
     seeds, targets, fan = hop2_slot.shape
-    half = (fan + 1) // 2
+    half = fan // 2 + 2
     step = (targets + 1) * seeds
     own_slot = target_slot.T
     near_slot = jnp.transpose(hop2_slot, (1, 2, 0))
@@ -346,7 +353,7 @@
             jax.ShapeDtypeStruct((owners * lines, LANES), jnp.float32),
             jax.ShapeDtypeStruct((peers, groups * (lines + cold_rows), width), jnp.bfloat16),
         ),
-        in_specs=[VMEM, VMEM, ANY, ANY, ANY],
+        in_specs=[ANY] * 5,
         out_specs=(ANY, ANY),
         scratch_shapes=[
             pltpu.VMEM((owners * lines, LANES), jnp.float32),
@@ -355,6 +362,8 @@
             pltpu.VMEM(cold_table.shape, jnp.float32),
             pltpu.VMEM(cold_table.shape, cold_table.dtype),
             pltpu.VMEM((cold_rows, width), jnp.float32),
+            pltpu.VMEM(own_slot.shape, jnp.int32),
+            pltpu.VMEM(near_slot.shape, jnp.int32),
             pltpu.SMEM(serve_index.shape, jnp.int32),
             pltpu.SMEM(serve_count.shape, jnp.int32),
             pltpu.SemaphoreType.DMA((8,)),
@@ -410,7 +419,7 @@
     return pl.pallas_call(
         functools.partial(finish_kernel, half, targets),
         out_shape=jax.ShapeDtypeStruct((seeds, w_second.shape[1]), jnp.float32),
-        in_specs=[ANY] * 5 + [ANY, VMEM, ANY, VMEM] + [VMEM] * (1 + groups),
+        in_specs=[ANY] * 10 + [VMEM] * groups,
         out_specs=VMEM,
         scratch_shapes=[
             pltpu.VMEM((rows + 8, width), jnp.float32),
@@ -423,14 +432,17 @@
             pltpu.SMEM((step,), jnp.int32),
             pltpu.SMEM((2,), jnp.int32),
             pltpu.VMEM((seeds, LANES), jnp.float32),
-            pltpu.SemaphoreType.DMA((8,)),
+            pltpu.VMEM((1, b_first.shape[0]), b_first.dtype),
+            pltpu.VMEM((1, b_second.shape[0]), b_second.dtype),
+            pltpu.VMEM((peers * cold_rows, width), hot_cache.dtype),
+            pltpu.SemaphoreType.DMA((11,)),
         ],
         name="finish",
     )(
         slots.reshape(-1), first, second, sizes, counts,
-        w_first, b_first[None], w_second, b_second[None],
+        w_first, b_first[None], w_second, b_second[None], colds[0].reshape(-1, width),
         in_vmem(received.reshape(owners * HOT_REQ, width)),
-        colds[0].reshape(-1, width), *(in_vmem(c.reshape(-1, width)) for c in colds[1:]),
+        *(in_vmem(c.reshape(-1, width)) for c in colds[1:]),
     )
 
 

time: 56.8 us -> 56.5 us (level)
  no operation moved by 1% of the time
where the time goes in v7:
time: 56.5 us; the launch traced here: 56 us
  Pallas kernels  27.6 us (49%)
  starting transfers between devices  19.2 us (34%)
  waiting for transfers between devices  9.13 us (16%)
    pallas_call x1, Pallas kernels, forward(): pl.pallas_call(functools.partial(finish_kernel, half, targets), out_shape...  11.1 us
    ppermute x3, waiting for transfers between devices, forward(): shards.append(lax.ppermute(hot_cache, 'gx', swaps[g]))  9.12 us
    ppermute x3, starting transfers between devices, forward(): colds[g] = lax.ppermute(colds[g], 'gx', swaps[g])  5.71 us
    all_to_all x1, starting transfers between devices, forward(): lax.all_to_all(ask, 'gx', split_axis=0, concat_axis=0, axis_index_groups=...  5.21 us
    pallas_call x1, Pallas kernels, forward(): pl.pallas_call(rank_kernel, out_shape=(jax.ShapeDtypeStruct((owners * lin...  5.12 us
    pallas_call x1, Pallas kernels, forward(): pl.pallas_call(functools.partial(remap_kernel, peers, owners, cold_rows,...  5.1 us
    pallas_call x1, Pallas kernels, forward(): pl.pallas_call(plan_kernel, out_shape=(jax.ShapeDtypeStruct((step,), jnp....  4.79 us
    ppermute x3, starting transfers between devices, forward(): shards.append(lax.ppermute(hot_cache, 'gx', swaps[g]))  4.45 us
  transfers between devices with their start and end apart: 8, of which 2 were waited for; matrix products, arithmetic and copies ran while one was open for 0% of the time, Pallas kernels for 18%

profile of v7, /device:TPU:0, one launch (start us, length us, event | category | flops | bytes accessed | tf_op | source)
XLA Modules:
  0.0 56.0 jit_solution(4202655746683855697)
XLA Ops:
  0.0 0.0 copy-start
  0.0 5.1 %rank.1 = (f32[128,128]{1,0:T(8,128)}, bf16[8,144,128]{2,1,0:T(8,128)(2,1)}) custom-call(s32[11,128]{1,0:T(8,128)} %bitcast.21, s32[11,15,128]{2,1,0:T(8,128)} %bitcast.17, s32[1,32,32]{2,1,0:T(8,128)} %wanted_in.1, s32[1,32]{1,0:T(1,128)} %live_in.1, bf16[8192,128]{1,0:T(8,128)(2,1)} %table.1), custom_call_target="tpu_custom_call" | custom-call | tf_op jit(solution)/shard_map/rank/pallas_call | solution.py:350
  5.1 5.2 %all-to-all-start = ((bf16[8,144,128]{2,1,0:T(8,128)(2,1)}), bf16[8,144,128]{2,1,0:T(8,128)(2,1)S(1)}, u32[]{:S(2)}, u32[]{:S(2)}) async-start(bf16[8,144,128]{2,1,0:T(8,128)(2,1)} %get-tuple-element.25), calls=%async_computation | async-start | bytes 589824 | tf_op jit(solution)/shard_map/all_to_all | solution.py:374
  10.3 0.0 copy-done
  10.3 2.7 %collective-permute-start.1 = (bf16[512,128]{1,0:T(8,128)(2,1)S(1)}, bf16[512,128]{1,0:T(8,128)(2,1)S(1)}, u32[]{:S(2)}, u32[]{:S(2)}) collective-permute-start(bf16[512,128]{1,0:T(8,128)(2,1)S(1)} %copy-done), channel_id=1, source_target_pairs={{0,16},{1,17},{2,18},{3,19},{4,20},{5,21},{6,22},{7,23},{8,24},{9,... | collective-permute-start | bytes 393224 | tf_op jit(solution)/shard_map/ppermute | solution.py:349
  13.0 1.6 %collective-permute-start = (bf16[512,128]{1,0:T(8,128)(2,1)S(1)}, bf16[512,128]{1,0:T(8,128)(2,1)S(1)}, u32[]{:S(2)}, u32[]{:S(2)}) collective-permute-start(bf16[512,128]{1,0:T(8,128)(2,1)S(1)} %copy-done), channel_id=1, source_target_pairs={{0,8},{1,9},{2,10},{3,11},{4,12},{5,13},{6,14},{7,15},{8,0},{9,1},... | collective-permute-start | bytes 393224 | tf_op jit(solution)/shard_map/ppermute | solution.py:349
  14.6 0.2 collective-permute-start.2
  14.8 5.7 %collective-permute-done.1.refs_2_ = bf16[512,128]{1,0:T(8,128)(2,1)S(1)} collective-permute-done((bf16[512,128]{1,0:T(8,128)(2,1)S(1)}, bf16[512,128]{1,0:T(8,128)(2,1)S(1)}, u32[]{:S(2)}, u32[]{:S(2)}) %collective-permute-start.1) | collective-permute-done | bytes 131104 | tf_op jit(solution)/shard_map/ppermute | solution.py:349
  20.5 0.0 collective-permute-done.refs_1_
  20.5 3.4 %collective-permute-done.2.refs_3_ = bf16[512,128]{1,0:T(8,128)(2,1)S(1)} collective-permute-done((bf16[512,128]{1,0:T(8,128)(2,1)S(1)}, bf16[512,128]{1,0:T(8,128)(2,1)S(1)}, u32[]{:S(2)}, u32[]{:S(2)}) %collective-permute-start.2) | collective-permute-done | bytes 131104 | tf_op jit(solution)/shard_map/ppermute | solution.py:349
  23.9 0.0 all-to-all-done.asked
  23.9 1.5 %select.1 = (bf16[8,256,128]{2,1,0:T(8,128)(2,1)}, bf16[8,32,128]{2,1,0:T(8,128)(2,1)}, bf16[8,32,128]{2,1,0:T(8,128)(2,1)}, bf16[8,32,128]{2,1,0:T(8,128)(2,1)}, bf16[8,32,128]{2,1,0:T(8,128)(2,1)}) custom-call(bf16[8,144,128]{2,1,0:T(8,128)(2,1)S(1)} %all-to-all-done.asked, bf16[512,128]{1,0:T(8,128)(2,1)S(1)} %copy-done, ...), custom_call_target="tpu_custom_call" | custom-call | tf_op jit(solution)/shard_map/select/pallas_call | solution.py:377
  25.4 3.8 %all-to-all-start.1 = ((bf16[8,256,128]{2,1,0:T(8,128)(2,1)}), bf16[8,256,128]{2,1,0:T(8,128)(2,1)S(1)}, u32[]{:S(2)}, u32[]{:S(2)}) async-start(bf16[8,256,128]{2,1,0:T(8,128)(2,1)} %get-tuple-element.27), calls=%async_computation.1 | async-start | bytes 1048576 | tf_op jit(solution)/shard_map/all_to_all | solution.py:389
  29.3 2.3 %collective-permute-start.3 = (bf16[8,32,128]{2,1,0:T(8,128)(2,1)}, bf16[8,32,128]{2,1,0:T(8,128)(2,1)S(1)}, u32[]{:S(2)}, u32[]{:S(2)}) collective-permute-start(bf16[8,32,128]{2,1,0:T(8,128)(2,1)} %get-tuple-element.28), channel_id=1, source_target_pairs={{0,8},{1,9},{2,10},{3,11},{4,12},{5,13},{6,14},{7,15},{8,0},{9,1},... | collective-permute-start | bytes 196616 | tf_op jit(solution)/shard_map/ppermute | solution.py:393
  31.6 2.0 %collective-permute-start.4 = (bf16[8,32,128]{2,1,0:T(8,128)(2,1)}, bf16[8,32,128]{2,1,0:T(8,128)(2,1)S(1)}, u32[]{:S(2)}, u32[]{:S(2)}) collective-permute-start(bf16[8,32,128]{2,1,0:T(8,128)(2,1)} %get-tuple-element.29), channel_id=1, source_target_pairs={{0,16},{1,17},{2,18},{3,19},{4,20},{5,21},{6,22},{7,23},{8,24},{9,... | collective-permute-start | bytes 196616 | tf_op jit(solution)/shard_map/ppermute | solution.py:393
  33.6 1.4 %collective-permute-start.5 = (bf16[8,32,128]{2,1,0:T(8,128)(2,1)}, bf16[8,32,128]{2,1,0:T(8,128)(2,1)S(1)}, u32[]{:S(2)}, u32[]{:S(2)}) collective-permute-start(bf16[8,32,128]{2,1,0:T(8,128)(2,1)} %get-tuple-element.30), channel_id=1, source_target_pairs={{0,24},{1,25},{2,26},{3,27},{4,28},{5,29},{6,30},{7,31},{8,16},{9,... | collective-permute-start | bytes 196616 | tf_op jit(solution)/shard_map/ppermute | solution.py:393
  35.0 5.1 %remap.1 = (s32[192,128]{1,0:T(8,128)}, s32[11,128]{1,0:T(8,128)}, f32[128,128]{1,0:T(8,128)}) custom-call(s32[11,128]{1,0:T(8,128)} %bitcast.22, s32[11,15,128]{2,1,0:T(8,128)} %bitcast.18, s32[11,128]{1,0:T(8,128)} %bitcast.24, s32[1,128]{1,0:T(1,128)} %bitcast.25, f32[128,128]{1,0:T(8,128)} %get-tuple-element.18.rank), custom_call_target="tpu_custom_call" | custom-call | tf_op jit(solution)/shard_map/remap/pallas_call | solution.py:395
  40.1 4.8 %plan.1 = (s32[1536]{0:T(1024)}, s32[1536]{0:T(1024)}, s32[2]{0:T(128)}) custom-call(s32[128]{0:T(128)} %hop1.1, s32[1408]{0:T(1024)} %bitcast.23), custom_call_target="tpu_custom_call" | custom-call | tf_op jit(solution)/shard_map/plan/pallas_call | solution.py:406
  44.9 0.0 collective-permute-done.3
  44.9 0.0 collective-permute-done.4
  44.9 0.0 collective-permute-done.5
  44.9 0.0 all-to-all-done.1
  44.9 11.1 %finish.1 = f32[128,256]{1,0:T(8,128)} custom-call(s32[24576]{0:T(1024)} %bitcast.19, s32[1536]{0:T(1024)} %get-tuple-element.21.first_in, s32[1536]{0:T(1024)} %get-tuple-element.22.second_in, s32[2]{0:T(128)} %get-tuple-element.23.sizes_in, f32[128,128]{1,0:T(8,128)} %get-tuple-element.24.counts_in, bf16[256,256]{1,0:T(8,128)(2,1)} %w_first_in.1, ...), custom_call_target="tpu_custom_call" | custom-call | tf_op jit(solution)/shard_map/finish/pallas_call | solution.py:419
Async XLA Ops:
  0.0 10.3 %copy-start = (bf16[512,128]{1,0:T(8,128)(2,1)S(1)}, bf16[512,128]{1,0:T(8,128)(2,1)}, u32[]{:S(2)}) copy-start(bf16[512,128]{1,0:T(8,128)(2,1)} %refs_0_.1) | copy-start | bytes 393220
  5.1 18.8 %all-to-all-start = ((bf16[8,144,128]{2,1,0:T(8,128)(2,1)}), bf16[8,144,128]{2,1,0:T(8,128)(2,1)S(1)}, u32[]{:S(2)}, u32[]{:S(2)}) async-start(bf16[8,144,128]{2,1,0:T(8,128)(2,1)} %get-tuple-element.25), calls=%async_computation | async-start | bytes 589824 | tf_op jit(solution)/shard_map/all_to_all | solution.py:374
  10.3 10.2 %collective-permute-start.1 = (bf16[512,128]{1,0:T(8,128)(2,1)S(1)}, bf16[512,128]{1,0:T(8,128)(2,1)S(1)}, u32[]{:S(2)}, u32[]{:S(2)}) collective-permute-start(bf16[512,128]{1,0:T(8,128)(2,1)S(1)} %copy-done), channel_id=1, source_target_pairs={{0,16},{1,17},{2,18},{3,19},{4,20},{5,21},{6,22},{7,23},{8,24},{9,... | collective-permute-start | bytes 393224 | tf_op jit(solution)/shard_map/ppermute | solution.py:349
  13.0 7.5 %collective-permute-start = (bf16[512,128]{1,0:T(8,128)(2,1)S(1)}, bf16[512,128]{1,0:T(8,128)(2,1)S(1)}, u32[]{:S(2)}, u32[]{:S(2)}) collective-permute-start(bf16[512,128]{1,0:T(8,128)(2,1)S(1)} %copy-done), channel_id=1, source_target_pairs={{0,8},{1,9},{2,10},{3,11},{4,12},{5,13},{6,14},{7,15},{8,0},{9,1},... | collective-permute-start | bytes 393224 | tf_op jit(solution)/shard_map/ppermute | solution.py:349
  14.6 9.3 %collective-permute-start.2 = (bf16[512,128]{1,0:T(8,128)(2,1)S(1)}, bf16[512,128]{1,0:T(8,128)(2,1)S(1)}, u32[]{:S(2)}, u32[]{:S(2)}) collective-permute-start(bf16[512,128]{1,0:T(8,128)(2,1)S(1)} %copy-done), channel_id=1, source_target_pairs={{0,24},{1,25},{2,26},{3,27},{4,28},{5,29},{6,30},{7,31},{8,16},{9,... | collective-permute-start | bytes 393224 | tf_op jit(solution)/shard_map/ppermute | solution.py:349
  25.4 19.5 %all-to-all-start.1 = ((bf16[8,256,128]{2,1,0:T(8,128)(2,1)}), bf16[8,256,128]{2,1,0:T(8,128)(2,1)S(1)}, u32[]{:S(2)}, u32[]{:S(2)}) async-start(bf16[8,256,128]{2,1,0:T(8,128)(2,1)} %get-tuple-element.27), calls=%async_computation.1 | async-start | bytes 1048576 | tf_op jit(solution)/shard_map/all_to_all | solution.py:389
  29.3 15.6 %collective-permute-start.3 = (bf16[8,32,128]{2,1,0:T(8,128)(2,1)}, bf16[8,32,128]{2,1,0:T(8,128)(2,1)S(1)}, u32[]{:S(2)}, u32[]{:S(2)}) collective-permute-start(bf16[8,32,128]{2,1,0:T(8,128)(2,1)} %get-tuple-element.28), channel_id=1, source_target_pairs={{0,8},{1,9},{2,10},{3,11},{4,12},{5,13},{6,14},{7,15},{8,0},{9,1},... | collective-permute-start | bytes 196616 | tf_op jit(solution)/shard_map/ppermute | solution.py:393
  31.6 13.3 %collective-permute-start.4 = (bf16[8,32,128]{2,1,0:T(8,128)(2,1)}, bf16[8,32,128]{2,1,0:T(8,128)(2,1)S(1)}, u32[]{:S(2)}, u32[]{:S(2)}) collective-permute-start(bf16[8,32,128]{2,1,0:T(8,128)(2,1)} %get-tuple-element.29), channel_id=1, source_target_pairs={{0,16},{1,17},{2,18},{3,19},{4,20},{5,21},{6,22},{7,23},{8,24},{9,... | collective-permute-start | bytes 196616 | tf_op jit(solution)/shard_map/ppermute | solution.py:393
  33.6 11.3 %collective-permute-start.5 = (bf16[8,32,128]{2,1,0:T(8,128)(2,1)}, bf16[8,32,128]{2,1,0:T(8,128)(2,1)S(1)}, u32[]{:S(2)}, u32[]{:S(2)}) collective-permute-start(bf16[8,32,128]{2,1,0:T(8,128)(2,1)} %get-tuple-element.30), channel_id=1, source_target_pairs={{0,24},{1,25},{2,26},{3,27},{4,28},{5,29},{6,30},{7,31},{8,16},{9,... | collective-permute-start | bytes 196616 | tf_op jit(solution)/shard_map/ppermute | solution.py:393
